TPU v7x, 32 devices: a whole 2x2x4 slice. The times are simulated.
32 devices in a mesh: dp: 16 (over z, x, core), tensor: 2 (over y).
Axes of the slice: x: 2, y: 2, z: 4, core: 2. Of those that a mesh axis runs over, the one named last changes fastest.
Arguments:
- tokens: bfloat16 [32768, 768], P('dp'), may hold values from -6 to 6
- lengths: int32 [64], P('dp'), may hold values from 64 to 512, as said below
- w_qkv: bfloat16 [768, 3, 768], P(None, None, 'tensor'), may hold values from -0.21875 to 0.21875
- q_bias: float32 [768], P('tensor'), may hold values from -3 to 3
- v_bias: float32 [768], P('tensor'), may hold values from -3 to 3
- w_out: bfloat16 [768, 768], P('tensor'), may hold values from -0.875 to 0.875
- out_bias: float32 [768], replicated, may hold values from -2 to 2
- gain_one: float32 [768], replicated, may hold values from 0.5 to 1.5
- shift_one: float32 [768], replicated, may hold values from -2 to 2
- w_in: bfloat16 [768, 3072], P(None, 'tensor'), may hold values from -0.21875 to 0.21875
- in_bias: float32 [3072], P('tensor'), may hold values from -3 to 3
- w_down: bfloat16 [3072, 768], P('tensor'), may hold values from -0.15625 to 0.15625
- down_bias: float32 [768], replicated, may hold values from -2 to 2
- gain_two: float32 [768], replicated, may hold values from 0.5 to 1.5
- shift_two: float32 [768], replicated, may hold values from -2 to 2
- cotangent: bfloat16 [32768, 768], P(('dp', 'tensor')), may hold values from -6 to 6
Outputs:
- output: bfloat16 [32768, 768], P(('dp', 'tensor'))
- input_grad: bfloat16 [32768, 768], P(('dp', 'tensor'))
- grad_w_qkv: float32 [768, 3, 768], P(None, None, 'tensor')
- grad_q_bias: float32 [768], P('tensor')
- grad_v_bias: float32 [768], P('tensor')
- grad_w_out: float32 [768, 768], P('tensor')
- grad_out_bias: float32 [768], replicated
- grad_gain_one: float32 [768], replicated
- grad_shift_one: float32 [768], replicated
- grad_w_in: float32 [768, 3072], P(None, 'tensor')
- grad_in_bias: float32 [3072], P('tensor')
- grad_w_down: float32 [3072, 768], P('tensor')
- grad_down_bias: float32 [768], replicated
- grad_gain_two: float32 [768], replicated
- grad_shift_two: float32 [768], replicated
Inputs may be any that keep to these rules, and one draw needn't show every extreme that they name: `lengths`: each sequence's valid tokens are its first ones; at least one sequence has all 512 tokens valid.
All inputs are finite; a program needn't handle non-finite values.
Results may differ from a plain program's by a relative error of at most 0.015.
Values may be sent and summed in bfloat16 or wider, within the bound.
No kernel may reach another device: no remote copies, remote signals or barrier semaphores. Data moves between devices by JAX's collectives and lax.ppermute only.
A program may use at most 192 MiB of HBM per device.

v0:
```python
import jax
import jax.numpy as jnp
from jax import lax
from jax.experimental import pallas as pl
from jax.experimental.pallas import tpu as pltpu
from jax.sharding import PartitionSpec as P

HEAD_DIM = 64
EPSILON = 1e-06
MASKED = -1000000000.0
LOW = jnp.bfloat16
WIDE = jnp.float32
RSQRT2PI = 0.3989422804014327


def contract(a, b, dim_a, dim_b):
    return lax.dot_general(
        a, b, (((dim_a,), (dim_b,)), ((), ())), preferred_element_type=WIDE
    )


def swap(array, bit, size):
    return lax.ppermute(array, "dp", [(i, i ^ (1 << bit)) for i in range(size)])


def across(array):
    return lax.ppermute(array, "tensor", [(0, 1), (1, 0)])


ANYWHERE = pl.BlockSpec(memory_space=pl.ANY)


def small_cost(flops=10**6):
    return pl.CostEstimate(flops=flops, bytes_accessed=10**5, transcendentals=0)


def attend_kernel(bits_ref, length_ref, q_ref, k_ref, v_ref, context_ref, probs_ref):
    length = length_ref[bits_ref[3] * pl.num_programs(0) + pl.program_id(0)]
    rows = q_ref.shape[0]
    lane = lax.broadcasted_iota(jnp.int32, (rows, 128), 1)
    slot = lax.broadcasted_iota(jnp.int32, (rows, 128), 0)
    masked = jnp.where(slot < length, 0.0, MASKED).astype(LOW)
    q, k, v = q_ref[...], k_ref[...], v_ref[...]
    zero, one = jnp.zeros_like(q), jnp.ones_like(q)
    contexts = []
    for head in range(2):
        mine = (lane >= 64) if head else (lane < 64)
        mark = lane == (0 if head else 64)
        k_head = jnp.where(mine, k, jnp.where(mark, masked, zero))
        q_head = jnp.where(mine, q, jnp.where(mark, one, zero))
        scores = contract(k_head, q_head, 1, 1)
        top = jnp.max(scores, axis=0, keepdims=True)
        exponent = jnp.exp(scores - top)
        total = jnp.sum(exponent, axis=0, keepdims=True)
        probs = (exponent * (1.0 / total)).astype(LOW)
        probs_ref[head] = probs
        contexts.append(contract(probs, v, 0, 0))
    context_ref[...] = jnp.where(lane < 64, contexts[0], contexts[1]).astype(LOW)


def attend(bits, lengths, q, k, v):
    rows, width = q.shape
    sequences = lengths.shape[0] // 2
    length, pairs = rows // sequences, width // 128
    block = pl.BlockSpec((length, 128), lambda s, h, *_: (s, h))
    return pl.pallas_call(
        attend_kernel,
        grid_spec=pltpu.PrefetchScalarGridSpec(
            num_scalar_prefetch=2,
            grid=(sequences, pairs),
            in_specs=[block] * 3,
            out_specs=[
                block,
                pl.BlockSpec((2, length, length), lambda s, h, *_: (s * pairs + h, 0, 0)),
            ],
        ),
        out_shape=[
            jax.ShapeDtypeStruct((rows, width), LOW),
            jax.ShapeDtypeStruct((sequences * pairs * 2, length, length), LOW),
        ],
        cost_estimate=small_cost(),
        name="attend",
    )(bits, lengths, q, k, v)


def attend_back_kernel(q_ref, k_ref, v_ref, context_ref, grad_ref, probs_ref, out_ref):
    rows = q_ref.shape[0]
    lane = lax.broadcasted_iota(jnp.int32, (rows, 128), 1)
    q, k, v, grad = q_ref[...], k_ref[...], v_ref[...], grad_ref[...]
    inner = pltpu.roll(grad.astype(WIDE) * context_ref[...].astype(WIDE), 64, 1).astype(LOW)
    zero, minus = jnp.zeros_like(q), -jnp.ones_like(q)
    grad_q = grad_k = grad_v = 0.0
    for head in range(2):
        mine = (lane >= 64) if head else (lane < 64)
        centred = contract(jnp.where(mine, v, minus), jnp.where(mine, grad, inner), 1, 1)
        probs = probs_ref[head]
        grad_scores = (probs.astype(WIDE) * centred).astype(LOW)
        grad_v += contract(probs, jnp.where(mine, grad, zero), 1, 0)
        grad_k += contract(grad_scores, jnp.where(mine, q, zero), 1, 0)
        grad_q += contract(grad_scores, jnp.where(mine, k, zero), 0, 0)
    out_ref[0] = (grad_q * HEAD_DIM**-0.5).astype(LOW)
    out_ref[1] = grad_k.astype(LOW)
    out_ref[2] = grad_v.astype(LOW)


def attend_back(q, k, v, context, grad, probs, sequences):
    rows, width = q.shape
    length, pairs = rows // sequences, width // 128
    block = pl.BlockSpec((length, 128), lambda s, h: (s, h))
    return pl.pallas_call(
        attend_back_kernel,
        grid=(sequences, pairs),
        in_specs=[block] * 5
        + [pl.BlockSpec((2, length, length), lambda s, h: (s * pairs + h, 0, 0))],
        out_specs=pl.BlockSpec((3, length, 128), lambda s, h: (0, s, h)),
        out_shape=jax.ShapeDtypeStruct((3, rows, width), LOW),
        cost_estimate=small_cost(),
        name="attend_back",
    )(q, k, v, context, grad, probs)


def pack_kernel(bits_ref, qkv_ref, out_ref, in_ref, down_ref, attention_ref, forward_ref):
    attention_ref[:3] = qkv_ref[...]
    for target, source in ((attention_ref.at[3], out_ref), (forward_ref, in_ref)):
        rows, width = source.shape[0], source.shape[1] // 2
        for side in range(2):
            target[side * rows : (side + 1) * rows] = source[:, side * width : (side + 1) * width]
    rows = down_ref.shape[0]
    forward_ref[rows:] = down_ref[...]


def pack(bits, w_qkv, w_out, w_in, w_down):
    quarters = [(3, w_qkv.shape[1] // 4, w_qkv.shape[2])]
    quarters += [(w.shape[0] // 4, w.shape[1]) for w in (w_out, w_in, w_down)]
    _, rows, local = quarters[0]
    attention, forward = (4, rows, local), (2 * quarters[3][0], quarters[3][1])

    def place(*index):
        return lambda i, s: tuple(s[0] * 2 + s[1] if k else 0 for k in index)

    return pl.pallas_call(
        pack_kernel,
        grid_spec=pltpu.PrefetchScalarGridSpec(
            num_scalar_prefetch=1,
            grid=(1,),
            in_specs=[pl.BlockSpec(quarters[0], place(0, 1, 0))]
            + [pl.BlockSpec(quarter, place(1, 0)) for quarter in quarters[1:]],
            out_specs=[pl.BlockSpec(attention, place(0, 0, 0)), pl.BlockSpec(forward, place(0, 0))],
        ),
        out_shape=[jax.ShapeDtypeStruct(attention, LOW), jax.ShapeDtypeStruct(forward, LOW)],
        cost_estimate=small_cost(),
        name="pack",
    )(bits, w_qkv, w_out, w_in, w_down)


class Order:
    def __init__(self, first):
        self.last = first

    def sync(self, *arrays):
        arrays, self.last = lax.optimization_barrier((arrays, self.last))
        return arrays

    def run(self, step, *arrays):
        arrays = self.sync(*arrays)
        result = step(*arrays)
        self.last = result[0] if isinstance(result, (list, tuple)) else result
        return result


class Fetch:
    def __init__(self, order, piece, size):
        self.order, self.size = order, size
        self.here = across(piece)

    def pass_on(self):
        (self.here,) = self.order.sync(self.here)
        self.x = swap(self.here, 1, self.size)
        self.partner = swap(self.here, 0, self.size)

    def finish(self):
        (self.x,) = self.order.sync(self.x)
        return [self.here, self.x, self.partner, swap(self.x, 0, self.size)]


def rank_of(bits_ref):
    return bits_ref[0] * 2 + bits_ref[1]


class Loads:
    def __init__(self, semaphores):
        self.semaphores, self.count, self.groups = semaphores, 0, []

    def group(self, pairs):
        copies = []
        for source, target in pairs:
            copies.append(pltpu.make_async_copy(source, target, self.semaphores.at[self.count]))
            self.count += 1
        self.groups.append(copies)
        return len(self.groups) - 1

    def start(self):
        @pl.when(pl.program_id(0) == 0)
        def _():
            for copies in self.groups:
                for copy in copies:
                    copy.start()

    def wait(self, group):
        @pl.when(pl.program_id(0) == 0)
        def _():
            for copy in self.groups[group]:
                copy.wait()


def qkv_parts(parts, target, rank):
    extent = target.shape[1] // 4
    return [
        (part.at[:3], target.at[:, pl.ds(pl.multiple_of((r ^ rank) * extent, 16), extent)])
        for r, part in enumerate(parts)
    ]


def out_parts(parts, target, rank):
    extent, width = target.shape[0] // 4, target.shape[1] // 2
    return [
        (
            part.at[3, pl.ds(side * extent, extent)],
            target.at[pl.ds(pl.multiple_of((r ^ rank) * extent, 16), extent), pl.ds(side * width, width)],
        )
        for r, part in enumerate(parts)
        for side in range(2)
    ]


def in_parts(parts, target, rank):
    extent, width = target.shape[0] // 4, target.shape[1] // 2
    return [
        (
            part.at[pl.ds(side * extent, extent)],
            target.at[pl.ds(pl.multiple_of((r ^ rank) * extent, 16), extent), pl.ds(side * width, width)],
        )
        for r, part in enumerate(parts)
        for side in range(2)
    ]


def down_parts(parts, target, rank):
    extent = target.shape[0] // 4
    return [
        (part.at[pl.ds(extent, extent)], target.at[pl.ds(pl.multiple_of((r ^ rank) * extent, 16), extent)])
        for r, part in enumerate(parts)
    ]


def project_kernel(bits_ref, x_ref, biases_ref, *refs):
    parts, (q_ref, k_ref, v_ref, weights, semaphores) = refs[:-5], refs[-5:]
    loads = Loads(semaphores)
    if len(parts) == 1:
        ready = loads.group([(parts[0], weights)])
    else:
        ready = loads.group(qkv_parts(parts, weights, rank_of(bits_ref)))
    loads.start()
    loads.wait(ready)
    x = x_ref[...]
    queries = (contract(x, weights[0], 1, 0) + biases_ref[0:1]).astype(LOW)
    q_ref[...] = queries * HEAD_DIM**-0.5
    k_ref[...] = contract(x, weights[1], 1, 0).astype(LOW)
    v_ref[...] = (contract(x, weights[2], 1, 0) + biases_ref[1:2]).astype(LOW)


def project(bits, tokens, biases, parts):
    rows, width = tokens.shape[0] // 2, tokens.shape[1]
    local = biases.shape[1]
    tile = 512
    steps = rows // tile
    return pl.pallas_call(
        project_kernel,
        grid_spec=pltpu.PrefetchScalarGridSpec(
            num_scalar_prefetch=1,
            grid=(steps,),
            in_specs=[
                pl.BlockSpec((tile, width), lambda i, s: (s[3] * steps + i, 0)),
                pl.BlockSpec(biases.shape, lambda i, s: (0, 0)),
            ]
            + [ANYWHERE] * len(parts),
            out_specs=[pl.BlockSpec((tile, local), lambda i, s: (i, 0))] * 3,
            scratch_shapes=[pltpu.VMEM((3, width, local), LOW), pltpu.SemaphoreType.DMA((4,))],
        ),
        out_shape=[jax.ShapeDtypeStruct((rows, local), LOW)] * 3,
        cost_estimate=small_cost(),
        name="project",
    )(bits, tokens, biases, *parts)


def project_back_kernel(bits_ref, own_ref, other_ref, grad_ref, weights_ref, *refs):
    parts, (out_ref, own_weights, other_weights, semaphores) = refs[:-4], refs[-4:]
    loads = Loads(semaphores)
    own_ready = loads.group([(weights_ref, own_weights)])
    other_ready = loads.group(qkv_parts(parts, other_weights, rank_of(bits_ref)))
    loads.start()
    loads.wait(own_ready)
    total = grad_ref[...].astype(WIDE)
    for index in range(3):
        total += contract(own_ref[index], own_weights[index], 1, 1)
    loads.wait(other_ready)
    for index in range(3):
        total += contract(other_ref[index], other_weights[index], 1, 1)
    out_ref[...] = total.astype(LOW)


def project_back(bits, own, other, grad, weights, parts):
    rows, width = grad.shape
    local = own.shape[2]
    tile = 256
    block = pl.BlockSpec((3, tile, local), lambda i, s: (0, i, 0))
    row_block = pl.BlockSpec((tile, width), lambda i, s: (i, 0))
    return pl.pallas_call(
        project_back_kernel,
        grid_spec=pltpu.PrefetchScalarGridSpec(
            num_scalar_prefetch=1,
            grid=(rows // tile,),
            in_specs=[block, block, row_block] + [ANYWHERE] * (1 + len(parts)),
            out_specs=row_block,
            scratch_shapes=[pltpu.VMEM((3, width, local), LOW)] * 2 + [pltpu.SemaphoreType.DMA((5,))],
        ),
        out_shape=jax.ShapeDtypeStruct((rows, width), LOW),
        cost_estimate=small_cost(),
        name="project_back",
    )(bits, own, other, grad, weights, *parts)


def normalize(values):
    average = jnp.mean(values, axis=-1, keepdims=True)
    centred = values - average
    scale = lax.rsqrt(jnp.mean(centred * centred, axis=-1, keepdims=True) + EPSILON)
    return centred * scale, scale


def normalize_back(grad, normed, scale, gain):
    grad_normed = grad * gain
    first = jnp.mean(grad_normed, axis=-1, keepdims=True)
    second = jnp.mean(grad_normed * normed, axis=-1, keepdims=True)
    return scale * (grad_normed - first - normed * second)


TAIL = (
    0.0356748104095459,
    -0.15720322728157043,
    0.20635373890399933,
    -0.053683843463659286,
    0.12856172025203705,
    0.09991346299648285,
    0.12075395882129669,
    0.11962930113077164,
)


def gelu_pair(values):
    t = 1.0 / (1.0 + 0.3 * jnp.abs(values))
    bell = jnp.exp(-0.5 * (values * values))
    series = TAIL[0]
    for coefficient in TAIL[1:]:
        series = series * t + coefficient
    tail = bell * (t * series)
    below = jnp.where(values < 0.0, tail, 1.0 - tail)
    return values * below, below + RSQRT2PI * (values * bell)


def in_bias_of(biases_ref):
    return jnp.concatenate([biases_ref[i : i + 1] for i in range(2, biases_ref.shape[0])], axis=1)


def first_kernel(
    bits_ref,
    own_context_ref,
    other_context_ref,
    x_ref,
    vectors_ref,
    biases_ref,
    w_out_ref,
    w_in_ref,
    w_down_ref,
    *refs,
):
    parts = refs[:4]
    hidden_ref, normed_ref, scale_ref, base_ref, act_ref, slope_ref = refs[4:10]
    own_out, other_out, w_in, w_down, semaphores = refs[10:]
    out_bias, gain, shift, down_bias = [vectors_ref[i : i + 1] for i in range(4)]
    loads = Loads(semaphores)
    out_ready = loads.group([(w_out_ref, own_out)] + out_parts(parts, other_out, rank_of(bits_ref)))
    in_ready = loads.group([(w_in_ref, w_in)])
    down_ready = loads.group([(w_down_ref, w_down)])
    loads.start()
    loads.wait(out_ready)
    pre_one = contract(own_context_ref[...], own_out[...], 1, 0)
    pre_one += contract(other_context_ref[...], other_out[...], 1, 0)
    pre_one += out_bias + x_ref[...].astype(WIDE)
    normed, scale = normalize(pre_one)
    hidden = normed * gain + shift
    hidden_low = hidden.astype(LOW)
    hidden_ref[...] = hidden_low
    normed_ref[...] = normed.astype(LOW)
    scale_ref[...] = scale
    loads.wait(in_ready)
    act, slope = gelu_pair(contract(hidden_low, w_in[...], 1, 0) + in_bias_of(biases_ref))
    act = act.astype(LOW)
    act_ref[...] = act
    slope_ref[...] = slope.astype(LOW)
    loads.wait(down_ready)
    base_ref[...] = hidden + down_bias + contract(act, w_down[...], 1, 0)


def first_half(bits, own_context, other_context, tokens, vectors, biases, w_out, w_in, w_down, parts):
    rows, local = own_context.shape
    width, hidden = w_in.shape
    tile = 256
    steps = rows // tile

    def row_block(columns):
        return pl.BlockSpec((tile, columns), lambda i, s: (i, 0))

    def whole(array):
        return pl.BlockSpec(array.shape, lambda i, s: (0, 0))

    return pl.pallas_call(
        first_kernel,
        grid_spec=pltpu.PrefetchScalarGridSpec(
            num_scalar_prefetch=1,
            grid=(rows // tile,),
            in_specs=[row_block(local), row_block(local)]
            + [pl.BlockSpec((tile, width), lambda i, s: (s[3] * steps + i, 0))]
            + [whole(vectors), whole(biases)]
            + [ANYWHERE] * (3 + len(parts)),
            out_specs=[
                row_block(width),
                row_block(width),
                row_block(1),
                row_block(width),
                row_block(hidden),
                row_block(hidden),
            ],
            scratch_shapes=[
                pltpu.VMEM((local, width), LOW),
                pltpu.VMEM((local, width), LOW),
                pltpu.VMEM((width, hidden), LOW),
                pltpu.VMEM((hidden, width), LOW),
                pltpu.SemaphoreType.DMA((11,)),
            ],
        ),
        out_shape=[
            jax.ShapeDtypeStruct((rows, width), LOW),
            jax.ShapeDtypeStruct((rows, width), LOW),
            jax.ShapeDtypeStruct((rows, 1), WIDE),
            jax.ShapeDtypeStruct((rows, width), WIDE),
            jax.ShapeDtypeStruct((rows, hidden), LOW),
            jax.ShapeDtypeStruct((rows, hidden), LOW),
        ],
        cost_estimate=small_cost(),
        name="first_half",
    )(bits, own_context, other_context, tokens, vectors, biases, w_out, w_in, w_down, *parts)


def second_kernel(
    bits_ref,
    hidden_ref,
    base_ref,
    cot_ref,
    slope_ref,
    normed_ref,
    scale_ref,
    vectors_ref,
    biases_ref,
    w_out_ref,
    w_in_ref,
    w_down_ref,
    *refs,
):
    out_pieces, pieces = refs[:4], refs[4:8]
    output_ref, branch_ref, act_ref, own_grad_ref, other_grad_ref, attended_ref = refs[8:14]
    own_context_ref, other_context_ref, sums_ref, bias_sums_ref = refs[14:18]
    own_out, other_out, own_in, other_in, own_down, other_down, semaphores = refs[18:]
    gain_one, gain_two, shift_two = vectors_ref[1:2], vectors_ref[4:5], vectors_ref[5:6]
    rank = rank_of(bits_ref)
    loads = Loads(semaphores)
    other_in_ready = loads.group(in_parts(pieces, other_in, rank))
    other_down_ready = loads.group(down_parts(pieces, other_down, rank))
    own_down_ready = loads.group([(w_down_ref, own_down)])
    own_in_ready = loads.group([(w_in_ref, own_in)])
    out_ready = loads.group([(w_out_ref, own_out)] + out_parts(out_pieces, other_out, rank))
    loads.start()

    @pl.when(pl.program_id(0) == 0)
    def _():
        sums_ref[...] = jnp.zeros_like(sums_ref)
        bias_sums_ref[...] = jnp.zeros_like(bias_sums_ref)

    def count(ref, row, values):
        ref[row : row + 1] += jnp.sum(values, axis=0, keepdims=True)

    loads.wait(other_in_ready)
    act, slope = gelu_pair(contract(hidden_ref[...], other_in[...], 1, 0) + in_bias_of(biases_ref))
    act = act.astype(LOW)
    act_ref[...] = act
    loads.wait(other_down_ready)
    pre_two = base_ref[...] + contract(act, other_down[...], 1, 0)
    normed, scale = normalize(pre_two)
    output_ref[...] = (normed * gain_two + shift_two).astype(LOW)
    cot = cot_ref[...].astype(WIDE)
    grad_pre_two = normalize_back(cot, normed, scale, gain_two)
    count(sums_ref, 4, cot * normed)
    count(sums_ref, 5, cot)
    count(sums_ref, 3, grad_pre_two)
    branch_grad = grad_pre_two.astype(LOW)
    branch_ref[...] = branch_grad
    grad = contract(branch_grad, other_down[...], 1, 1) * slope
    count(bias_sums_ref, 1, grad)
    grad = grad.astype(LOW)
    other_grad_ref[...] = grad
    grad_hidden = grad_pre_two + contract(grad, other_in[...], 1, 1)
    loads.wait(own_down_ready)
    grad = contract(branch_grad, own_down[...], 1, 1) * slope_ref[...].astype(WIDE)
    count(bias_sums_ref, 0, grad)
    grad = grad.astype(LOW)
    own_grad_ref[...] = grad
    loads.wait(own_in_ready)
    grad_hidden += contract(grad, own_in[...], 1, 1)
    normed = normed_ref[...].astype(WIDE)
    grad_pre_one = normalize_back(grad_hidden, normed, scale_ref[...], gain_one)
    count(sums_ref, 1, grad_hidden * normed)
    count(sums_ref, 2, grad_hidden)
    count(sums_ref, 0, grad_pre_one)
    attended = grad_pre_one.astype(LOW)
    attended_ref[...] = attended
    loads.wait(out_ready)
    own_context_ref[...] = contract(attended, own_out[...], 1, 1).astype(LOW)
    other_context_ref[...] = contract(attended, other_out[...], 1, 1).astype(LOW)


def second_half(bits, hidden_low, base, cot, slope, normed, scale, vectors, biases, w_out, w_in, w_down, out_pieces, pieces):
    rows, width = hidden_low.shape
    local, hidden = w_out.shape[0], w_in.shape[1]
    tile = 256

    def row_block(columns):
        return pl.BlockSpec((tile, columns), lambda i, s: (i, 0))

    def whole(columns, count=1):
        return pl.BlockSpec((count, columns), lambda i, s: (0, 0))

    def low(columns):
        return jax.ShapeDtypeStruct((rows, columns), LOW)

    return pl.pallas_call(
        second_kernel,
        grid_spec=pltpu.PrefetchScalarGridSpec(
            num_scalar_prefetch=1,
            grid=(rows // tile,),
            in_specs=[
                row_block(width),
                row_block(width),
                row_block(width),
                row_block(hidden),
                row_block(width),
                row_block(1),
            ]
            + [pl.BlockSpec(array.shape, lambda i, s: (0, 0)) for array in (vectors, biases)]
            + [ANYWHERE] * (3 + len(out_pieces) + len(pieces)),
            out_specs=[
                row_block(width),
                row_block(width),
                row_block(hidden),
                row_block(hidden),
                row_block(hidden),
                row_block(width),
                row_block(local),
                row_block(local),
                whole(width, 8),
                whole(hidden, 8),
            ],
            scratch_shapes=[
                pltpu.VMEM((local, width), LOW),
                pltpu.VMEM((local, width), LOW),
                pltpu.VMEM((width, hidden), LOW),
                pltpu.VMEM((width, hidden), LOW),
                pltpu.VMEM((hidden, width), LOW),
                pltpu.VMEM((hidden, width), LOW),
                pltpu.SemaphoreType.DMA((23,)),
            ],
        ),
        out_shape=[
            low(width),
            low(width),
            low(hidden),
            low(hidden),
            low(hidden),
            low(width),
            low(local),
            low(local),
            jax.ShapeDtypeStruct((8, width), WIDE),
            jax.ShapeDtypeStruct((8, hidden), WIDE),
        ],
        cost_estimate=small_cost(),
        name="second_half",
    )(bits, hidden_low, base, cot, slope, normed, scale, vectors, biases, w_out, w_in, w_down, *out_pieces, *pieces)


def down_kernel(bits_ref, act_ref, grad_ref, sent_ref, kept_ref):
    z = bits_ref[2]
    result = contract(act_ref[...], grad_ref[...], 0, 0)
    rows = result.shape[0] // 2

    def put(out_ref):
        for part in range(2):
            out_ref[0, part ^ z] = result[part * rows : (part + 1) * rows].astype(LOW)

    @pl.when(pl.program_id(0) < 2)
    def _():
        put(sent_ref)

    @pl.when(pl.program_id(0) >= 2)
    def _():
        put(kept_ref)


def down_pieces(bits, activated, grad):
    rows, hidden = activated.shape
    width = grad.shape[1]
    piece = (1, 2, hidden // 8, width)
    return pl.pallas_call(
        down_kernel,
        grid_spec=pltpu.PrefetchScalarGridSpec(
            num_scalar_prefetch=1,
            grid=(4,),
            in_specs=[
                pl.BlockSpec(
                    (rows, hidden // 4), lambda i, s: (0, (s[0] ^ (1 - i // 2)) * 2 + ((i % 2) ^ s[1]))
                ),
                pl.BlockSpec((rows, width), lambda i, s: (0, 0)),
            ],
            out_specs=[
                pl.BlockSpec(piece, lambda i, s: (jnp.minimum(i, 1), 0, 0, 0)),
                pl.BlockSpec(piece, lambda i, s: (jnp.maximum(i - 2, 0), 0, 0, 0)),
            ],
        ),
        out_shape=[jax.ShapeDtypeStruct((2,) + piece[1:], LOW)] * 2,
        cost_estimate=small_cost(),
        name="down_pieces",
    )(bits, activated, grad)


def in_kernel(bits_ref, hidden_ref, grad_ref, sent_ref, kept_ref):
    x, z = bits_ref[1], bits_ref[2]
    result = contract(hidden_ref[...], grad_ref[...], 0, 0)
    rows, columns = result.shape[0] // 2, result.shape[1] // 2

    def put(out_ref):
        for side in range(2):
            for part in range(2):
                out_ref[side ^ x, part ^ z] = result[
                    part * rows : (part + 1) * rows, side * columns : (side + 1) * columns
                ].astype(LOW)

    @pl.when(pl.program_id(0) == 0)
    def _():
        put(sent_ref)

    @pl.when(pl.program_id(0) == 1)
    def _():
        put(kept_ref)


def in_pieces(bits, hidden_low, grad):
    rows, width = hidden_low.shape
    hidden = grad.shape[1]
    piece = (2, 2, width // 2, hidden // 4)
    return pl.pallas_call(
        in_kernel,
        grid_spec=pltpu.PrefetchScalarGridSpec(
            num_scalar_prefetch=1,
            grid=(2,),
            in_specs=[
                pl.BlockSpec((rows, width), lambda i, s: (0, 0)),
                pl.BlockSpec((rows, hidden // 2), lambda i, s: (0, s[0] ^ (1 - i))),
            ],
            out_specs=[pl.BlockSpec(piece, lambda i, s: (0, 0, 0, 0))] * 2,
        ),
        out_shape=[jax.ShapeDtypeStruct(piece, LOW)] * 2,
        cost_estimate=small_cost(),
        name="in_pieces",
    )(bits, hidden_low, grad)


def heads_kernel(bits_ref, x_ref, grads_ref, context_ref, attended_ref, sent_ref, kept_ref, scratch):
    core = bits_ref[0]
    mine = bits_ref[1] * 2 + bits_ref[2]
    extent, local = scratch.shape[1:]

    @pl.when(pl.program_id(0) < 3)
    def _():
        result = contract(x_ref[...], grads_ref[0], 0, 0)
        for part in range(8):
            scratch[part] = result[part * extent : (part + 1) * extent]

    @pl.when(pl.program_id(0) == 3)
    def _():
        result = contract(context_ref[...], attended_ref[...], 0, 0)
        for part in range(8):
            rows, side = part % 4, part // 4
            scratch[part] = result[rows * extent : (rows + 1) * extent, side * local : (side + 1) * local]

    for part in range(4):
        sent_ref[part ^ mine, 0] = scratch[(1 - core) * 4 + part].astype(LOW)
        kept_ref[part ^ mine, 0] = scratch[core * 4 + part].astype(LOW)


def heads_pieces(bits, tokens, grads, context, attended):
    rows, local = context.shape
    width = tokens.shape[1]
    return pl.pallas_call(
        heads_kernel,
        grid_spec=pltpu.PrefetchScalarGridSpec(
            num_scalar_prefetch=1,
            grid=(4,),
            in_specs=[
                pl.BlockSpec((rows, width), lambda j, s: (s[3], 0)),
                pl.BlockSpec((1, rows, local), lambda j, s: (jnp.minimum(j, 2), 0, 0)),
                pl.BlockSpec((rows, local), lambda j, s: (0, 0)),
                pl.BlockSpec((rows, width), lambda j, s: (0, 0)),
            ],
            out_specs=[pl.BlockSpec((4, 1, width // 8, local), lambda j, s: (0, j, 0, 0))] * 2,
            scratch_shapes=[pltpu.VMEM((8, width // 8, local), WIDE)],
        ),
        out_shape=[jax.ShapeDtypeStruct((4, 4, width // 8, local), LOW)] * 2,
        cost_estimate=small_cost(),
        name="heads_pieces",
    )(bits, tokens, grads, context, attended)


def add(*arrays):
    total = arrays[0].astype(WIDE)
    for array in arrays[1:]:
        total = total + array.astype(WIDE)
    return total.astype(LOW)


class Chain:
    AXES = {"x": 1, "z": 2}

    def __init__(self, order, size):
        self.order, self.size = order, size
        self.terms = {"own": [], "other": []}

    def begin(self, side, sent, kept):
        for array in (kept, swap(sent, 0, self.size)):
            self.terms[side].append((array, (), ("x", "z")))

    def summed(self, terms):
        def cut(*arrays):
            parts = []
            for array, (_, picks, _) in zip(arrays, terms):
                for axis, index in picks:
                    array = lax.index_in_dim(array, index, axis, False)
                parts.append(array)
            return add(*parts)

        return self.order.run(cut, *[array for array, _, _ in terms])

    def halve(self, side, name):
        def pick(term, index):
            array, picks, axes = term
            if name not in axes:
                return term
            left = tuple(axis for axis in axes if axis != name)
            return array, picks + ((axes.index(name), index),), left

        terms = self.terms[side]
        there = [pick(term, 1) for term in terms if name in term[2]]
        arrived = swap(self.summed(there), self.AXES[name], self.size)
        self.terms[side] = [pick(term, 0) for term in terms] + [(arrived, (), there[0][2])]

    def cross(self):
        terms = self.terms["other"]
        self.terms["own"].append((across(self.summed(terms)), (), terms[0][2]))

    def total(self):
        self.kept = self.summed(self.terms["own"])

    def exchange(self, bit):
        self.terms["own"] = [(array, (), ()) for array in (self.kept, swap(self.kept, bit, self.size))]

    def spread(self):
        self.pieces = [self.kept] + [swap(self.kept, bit, self.size) for bit in (2, 1, 0)]

    def spread_on(self):
        kept, z, x, partner = self.pieces
        (z,) = self.order.sync(z)
        self.pieces = [kept, z, x, swap(z, 1, self.size), partner, swap(z, 0, self.size)]

    def finish(self):
        kept, z, x, xz, partner, partner_z = self.pieces
        x, xz = self.order.sync(x, xz)
        return [kept, z, x, xz, partner, partner_z, swap(x, 0, self.size), swap(xz, 0, self.size)]


def widen(bits, pieces, shapes, places):
    def kernel(bits_ref, *refs):
        sources, outs, (low, wide, semaphores) = refs[:8], refs[8:-3], refs[-3:]
        rank = bits_ref[0] * 4 + bits_ref[1] * 2 + bits_ref[2]
        loads = [pltpu.make_async_copy(sources[r], low.at[r], semaphores.at[r]) for r in range(8)]
        for load in loads:
            load.start()
        stores = []
        for r, load in enumerate(loads):
            load.wait()
            wide[r] = low[r].astype(WIDE)
            q = r ^ rank
            for part, target in places(q // 4, (q // 2) % 2, q % 2, wide.at[r], outs):
                stores.append(pltpu.make_async_copy(part, target, semaphores.at[8 + len(stores)]))
                stores[-1].start()
        for store in stores:
            store.wait()

    piece = pieces[0].shape
    return pl.pallas_call(
        kernel,
        grid_spec=pltpu.PrefetchScalarGridSpec(
            num_scalar_prefetch=1,
            grid=(1,),
            in_specs=[ANYWHERE] * 8,
            out_specs=[ANYWHERE] * len(shapes),
            scratch_shapes=[
                pltpu.VMEM((8,) + piece, LOW),
                pltpu.VMEM((8,) + piece, WIDE),
                pltpu.SemaphoreType.DMA((8 + 8 * len(shapes),)),
            ],
        ),
        out_shape=[jax.ShapeDtypeStruct(shape, WIDE) for shape in shapes],
        cost_estimate=small_cost(),
        name="widen",
    )(bits, *pieces)


def stretch(index, extent, unit):
    return pl.ds(pl.multiple_of(index * extent, unit), extent)


def down_places(core, x, z, piece, outs):
    return [(piece, outs[0].at[stretch(core * 4 + x * 2 + z, piece.shape[0], 8)])]


def in_places(core, x, z, piece, outs):
    rows, columns = piece.shape
    return [(piece, outs[0].at[stretch(z, rows, 8), stretch(core * 2 + x, columns, 128)])]


def heads_places(core, x, z, piece, outs):
    _, rows, columns = piece.shape
    return [
        (piece.at[:3], outs[0].at[:, stretch(core * 4 + x * 2 + z, rows, 8)]),
        (piece.at[3], outs[1].at[stretch(x * 2 + z, rows, 8), stretch(core, columns, 128)]),
    ]


def body(
    tokens,
    lengths,
    w_qkv,
    q_bias,
    v_bias,
    w_out,
    out_bias,
    gain_one,
    shift_one,
    w_in,
    in_bias,
    w_down,
    down_bias,
    gain_two,
    shift_two,
    cotangent,
):
    width, hidden = w_in.shape
    local = w_qkv.shape[2]
    sequences = lengths.shape[0] // 2
    size = lax.axis_size("dp")
    extra = range(3, size.bit_length() - 1)
    dp = lax.axis_index("dp")
    bits = jnp.stack([dp & 1, (dp >> 1) & 1, (dp >> 2) & 1, lax.axis_index("tensor")]).astype(jnp.int32)

    qkv_own = jnp.transpose(w_qkv, (1, 0, 2))
    attention_piece, forward_piece = pack(bits, qkv_own, w_out, w_in, w_down)
    order = Order(attention_piece)
    attention_fetch = Fetch(order, attention_piece, size)
    biases = order.run(
        lambda *vectors: jnp.concatenate([v.reshape(-1, local) for v in vectors]), q_bias, v_bias, in_bias
    )
    vectors = order.run(
        lambda *vectors: jnp.stack(vectors), out_bias, gain_one, shift_one, down_bias, gain_two, shift_two
    )
    biases_other = across(biases)
    (forward_piece,) = order.sync(forward_piece)
    forward_fetch = Fetch(order, forward_piece, size)

    q_own, k_own, v_own = order.run(lambda x: project(bits, x, biases, [qkv_own]), tokens)
    attention_fetch.pass_on()
    context_own, probs_own = order.run(
        lambda *qkv: attend(bits, lengths, *qkv), q_own, k_own, v_own
    )
    attention_pieces = attention_fetch.finish()
    q_other, k_other, v_other = order.run(
        lambda biases, *parts: project(bits, tokens, biases, parts), biases_other, *attention_pieces
    )
    forward_fetch.pass_on()
    context_other, probs_other = order.run(
        lambda *qkv: attend(bits, lengths, *qkv), q_other, k_other, v_other
    )
    hidden_low, normed_one, scale_one, base, act_own, slope_own = order.run(
        lambda own, other: first_half(
            bits, own, other, tokens, vectors, biases, w_out, w_in, w_down, attention_pieces
        ),
        context_own,
        context_other,
    )
    forward_pieces = forward_fetch.finish()
    (
        output,
        branch_grad,
        act_other,
        grad_own,
        grad_other,
        attended_grad,
        context_grad_own,
        context_grad_other,
        sums,
        bias_sums,
    ) = order.run(
        lambda hidden_low, *pieces: second_half(
            bits,
            hidden_low,
            base,
            cotangent,
            slope_own,
            normed_one,
            scale_one,
            vectors,
            biases_other,
            w_out,
            w_in,
            w_down,
            attention_pieces,
            pieces,
        ),
        hidden_low,
        *forward_pieces,
    )

    down, entry, heads = Chain(order, size), Chain(order, size), Chain(order, size)

    def down_grad(act):
        return order.run(lambda act: down_pieces(bits, act, branch_grad), act)

    def in_grad(grad):
        return order.run(lambda grad: in_pieces(bits, hidden_low, grad), grad)

    def heads_back(q, k, v, context, context_grad, probs):
        return order.run(
            lambda *args: attend_back(*args, sequences), q, k, v, context, context_grad, probs
        )

    def heads_grad(grads, context):
        pieces = order.run(
            lambda grads: heads_pieces(bits, tokens, grads, context, attended_grad), grads
        )
        return [piece.reshape(2, 2, *piece.shape[1:]) for piece in pieces]

    def head_sums(grads):
        return [jnp.sum(grads[0].astype(WIDE), axis=0), jnp.sum(grads[2].astype(WIDE), axis=0)]

    down.begin("other", *down_grad(act_other))
    entry.begin("other", *in_grad(grad_other))
    down.cross()
    entry.begin("own", *in_grad(grad_own))
    entry.halve("other", "x")
    down.begin("own", *down_grad(act_own))
    project_other = heads_back(
        q_other, k_other, v_other, context_other, context_grad_other, probs_other
    )
    entry.halve("own", "x")
    entry.cross()
    down.halve("own", "x")
    heads.begin("other", *heads_grad(project_other, context_other))
    other_sums = order.run(
        lambda grads, sums: jnp.concatenate([sums[:6].reshape(-1), bias_sums[1]] + head_sums(grads)),
        project_other,
        sums,
    )
    heads.cross()
    project_own = heads_back(q_own, k_own, v_own, context_own, context_grad_own, probs_own)
    entry.halve("own", "z")
    down.halve("own", "z")
    heads.begin("own", *heads_grad(project_own, context_own))
    arrived = across(other_sums)
    entry.total()
    if extra:
        entry.exchange(extra[0])
    down.total()
    if extra:
        down.exchange(extra[0])
    input_grad = order.run(
        lambda *grads: project_back(bits, *grads, attended_grad, qkv_own, attention_pieces),
        project_own,
        project_other,
    )
    totals = order.run(
        lambda grads, sums, arrived: jnp.concatenate(
            [sums[:6].reshape(-1), bias_sums[0]] + head_sums(grads)
        )
        + arrived,
        project_own,
        sums,
        arrived,
    )
    arrived = swap(totals, 0, size)
    heads.halve("own", "x")
    totals = order.run(jnp.add, totals, arrived)
    arrived = swap(totals, 1, size)
    for bit in extra:
        entry.total()
        if bit + 1 in extra:
            entry.exchange(bit + 1)
        down.total()
        if bit + 1 in extra:
            down.exchange(bit + 1)
    entry.spread()
    down.spread()
    totals = order.run(jnp.add, totals, arrived)
    arrived = swap(totals, 2, size)
    heads.halve("own", "z")
    entry.spread_on()
    down.spread_on()
    totals = order.run(jnp.add, totals, arrived)
    heads.total()
    entry_pieces = entry.finish()
    down_pieces_all = down.finish()
    for bit in extra:
        heads.exchange(bit)
        arrived = swap(totals, bit, size)
        if bit == extra[0]:
            (grad_w_in,) = order.run(
                lambda *pieces: widen(bits, pieces, [(width, hidden)], in_places), *entry_pieces
            )
        totals = order.run(jnp.add, totals, arrived)
        heads.total()
    heads.spread()
    (grad_w_down,) = order.run(
        lambda *pieces: widen(bits, pieces, [(hidden, width)], down_places), *down_pieces_all
    )
    heads.spread_on()
    count = 6 * width
    shared = totals[:count].reshape(6, width)
    grad_in_bias = totals[count : count + hidden]
    head_biases = totals[count + hidden :]
    grad_qkv, grad_w_out = order.run(
        lambda *pieces: widen(bits, pieces, [(3, width, local), (local, width)], heads_places),
        *heads.finish(),
    )

    return (
        output,
        input_grad,
        jnp.transpose(grad_qkv, (1, 0, 2)),
        head_biases[:local],
        head_biases[local:],
        grad_w_out,
        shared[0],
        shared[1],
        shared[2],
        grad_w_in,
        grad_in_bias,
        grad_w_down,
        shared[3],
        shared[4],
        shared[5],
    )


def solution(mesh):
    placed = (
        P("dp", None),
        P("dp"),
        P(None, None, "tensor"),
        P("tensor"),
        P("tensor"),
        P("tensor", None),
        P(),
        P(),
        P(),
        P(None, "tensor"),
        P("tensor"),
        P("tensor", None),
        P(),
        P(),
        P(),
        P(("dp", "tensor"), None),
    )
    return jax.shard_map(
        body,
        mesh=mesh,
        in_specs=placed,
        out_specs=(
            P(("dp", "tensor"), None),
            P(("dp", "tensor"), None),
            P(None, None, "tensor"),
            P("tensor"),
            P("tensor"),
            P("tensor", None),
            P(),
            P(),
            P(),
            P(None, "tensor"),
            P("tensor"),
            P("tensor", None),
            P(),
            P(),
            P(),
        ),
        check_vma=False,
    )
```

profile of v0, /device:TPU:0, one launch (start us, length us, event | category | flops | bytes accessed | tf_op | source)
XLA Modules:
  0.0 369.9 jit_solution(3356332271054451236)
XLA Ops:
  1.3 3.5 pack.1
  4.8 3.0 collective-permute-start.1
  8.5 7.1 %project.2 = (bf16[1024,384]{1,0:T(8,128)(2,1)}, bf16[1024,384]{1,0:T(8,128)(2,1)}, bf16[1024,384]{1,0:T(8,128)(2,1)}) custom-call(s32[4]{0:T(128)} %pad_add_fusion.bits_ref, bf16[2048,768]{1,0:T(8,128)(2,1)} %x_ref.8, f32[6,384]{1,0:T(8,128)} %pad_maximum_fusion.1.biases_ref, bf16[3,768,384]{2,1,0:T(8,128)(2,1)} %bitcast.61), custom_call_target="tpu_custom_call" | custom-call | flops 1000000 | bytes 100000 | tf_op jit(solution)/shard_map/project/pallas_call | solution.py:277
  15.6 5.7 %collective-permute-done.1.refs_0_ = bf16[4,192,384]{2,1,0:T(8,128)(2,1)S(1)} collective-permute-done((bf16[4,192,384]{2,1,0:T(8,128)(2,1)}, bf16[4,192,384]{2,1,0:T(8,128)(2,1)S(1)}, u32[]{:S(2)}, u32[]{:S(2)}) %collective-permute-start.1) | collective-permute-done | bytes 589856 | tf_op jit(solution)/shard_map/ppermute | solution.py:27
  21.3 1.7 collective-permute-start.2
  25.3 10.7 %attend.2 = (bf16[1024,384]{1,0:T(8,128)(2,1)}, bf16[12,512,512]{2,1,0:T(8,128)(2,1)}) custom-call(s32[4]{0:T(128)} %pad_add_fusion.bits_ref, s32[4]{0:T(128)} %length_ref.3, bf16[1024,384]{1,0:T(8,128)(2,1)} %get-tuple-element.301.q_ref, bf16[1024,384]{1,0:T(8,128)(2,1)} %get-tuple-element.302.k_ref, bf16[1024,384]{1,0:T(8,128)(2,1)} %get-tuple-element.210.v_ref), custom_call_target="tpu_custom_call" | custom-call | flops 1000000 | bytes 100000 | tf_op jit(solution)/shard_map/attend/pallas_call | solution.py:66
  37.4 13.5 %collective-permute-done.biases_ref = f32[6,384]{1,0:T(8,128)S(1)} collective-permute-done((f32[6,384]{1,0:T(8,128)S(1)}, f32[6,384]{1,0:T(8,128)S(1)}, u32[]{:S(2)}, u32[]{:S(2)}) %collective-permute-start) | collective-permute-done | bytes 9248 | tf_op jit(solution)/shard_map/ppermute | solution.py:27
  53.1 7.1 %project.3 = (bf16[1024,384]{1,0:T(8,128)(2,1)}, bf16[1024,384]{1,0:T(8,128)(2,1)}, bf16[1024,384]{1,0:T(8,128)(2,1)}) custom-call(s32[4]{0:T(128)} %pad_add_fusion.bits_ref, bf16[2048,768]{1,0:T(8,128)(2,1)} %x_ref.8, f32[6,384]{1,0:T(8,128)} %copy-done.47, bf16[4,192,384]{2,1,0:T(8,128)(2,1)} %copy-done.2, bf16[4,192,384]{2,1,0:T(8,128)(2,1)} %copy-done.3, ...), custom_call_target="tpu_custom_call" | custom-call | flops 1000000 | bytes 100000 | tf_op jit(solution)/shard_map/project/pallas_call | solution.py:277
  60.9 10.6 %attend.3 = (bf16[1024,384]{1,0:T(8,128)(2,1)}, bf16[12,512,512]{2,1,0:T(8,128)(2,1)}) custom-call(s32[4]{0:T(128)} %pad_add_fusion.bits_ref, s32[4]{0:T(128)} %length_ref.3, bf16[1024,384]{1,0:T(8,128)(2,1)} %get-tuple-element.275.q_ref, bf16[1024,384]{1,0:T(8,128)(2,1)} %get-tuple-element.276.k_ref, bf16[1024,384]{1,0:T(8,128)(2,1)} %get-tuple-element.222.v_ref), custom_call_target="tpu_custom_call" | custom-call | flops 1000000 | bytes 100000 | tf_op jit(solution)/shard_map/attend/pallas_call | solution.py:66
  71.5 20.3 %first_half.1 = (bf16[1024,768]{1,0:T(8,128)(2,1)}, bf16[1024,768]{1,0:T(8,128)(2,1)}, f32[1024,1]{1,0:T(8,128)}, f32[1024,768]{1,0:T(8,128)}, bf16[1024,1536]{1,0:T(8,128)(2,1)}, /*index=5*/bf16[1024,1536]{1,0:T(8,128)(2,1)}) custom-call(s32[4]{0:T(128)} %pad_add_fusion.bits_ref, bf16[1024,384]{1,0:T(8,128)(2,1)} %get-tuple-element.304.own_context_ref.context_ref, ...), custom_call_target="tpu_custom_call" | custom-call | flops 1000000 | bytes 100000 | tf_op jit(solution)/shard_map/first_half/pallas_call | solution.py:426
  92.3 2.5 collective-permute-done.8.refs_7_
  95.8 39.0 %second_half.1 = (bf16[1024,768]{1,0:T(8,128)(2,1)}, bf16[1024,768]{1,0:T(8,128)(2,1)}, bf16[1024,1536]{1,0:T(8,128)(2,1)}, bf16[1024,1536]{1,0:T(8,128)(2,1)}, ...) custom-call(s32[4]{0:T(128)} %pad_add_fusion.bits_ref, ...), custom_call_target="tpu_custom_call" | custom-call | flops 1000000 | bytes 100000 | tf_op jit(solution)/shard_map/second_half/pallas_call | solution.py:554
  134.9 7.4 %down_pieces.2 = (bf16[2,2,192,768]{3,2,1,0:T(8,128)(2,1)}, bf16[2,2,192,768]{3,2,1,0:T(8,128)(2,1)}) custom-call(s32[4]{0:T(128)} %pad_add_fusion.bits_ref, bf16[1024,1536]{1,0:T(8,128)(2,1)} %get-tuple-element.259.act_ref, bf16[1024,768]{1,0:T(8,128)(2,1)} %get-tuple-element.260.grad_ref), custom_call_target="tpu_custom_call" | custom-call | flops 1000000 | bytes 100000 | tf_op jit(solution)/shard_map/down_pieces/pallas_call | solution.py:630
  142.7 7.2 %in_pieces.2 = (bf16[2,2,384,384]{3,2,1,0:T(8,128)(2,1)}, bf16[2,2,384,384]{3,2,1,0:T(8,128)(2,1)}) custom-call(s32[4]{0:T(128)} %pad_add_fusion.bits_ref, bf16[1024,768]{1,0:T(8,128)(2,1)} %get-tuple-element.238.hidden_ref, bf16[1024,1536]{1,0:T(8,128)(2,1)} %get-tuple-element.262.grad_ref), custom_call_target="tpu_custom_call" | custom-call | flops 1000000 | bytes 100000 | tf_op jit(solution)/shard_map/in_pieces/pallas_call | solution.py:677
  150.4 7.3 %in_pieces.3 = (bf16[2,2,384,384]{3,2,1,0:T(8,128)(2,1)}, bf16[2,2,384,384]{3,2,1,0:T(8,128)(2,1)}) custom-call(s32[4]{0:T(128)} %pad_add_fusion.bits_ref, bf16[1024,768]{1,0:T(8,128)(2,1)} %get-tuple-element.238.hidden_ref, bf16[1024,1536]{1,0:T(8,128)(2,1)} %get-tuple-element.269.grad_ref), custom_call_target="tpu_custom_call" | custom-call | flops 1000000 | bytes 100000 | tf_op jit(solution)/shard_map/in_pieces/pallas_call | solution.py:677
  158.0 2.0 fusion.1
  160.0 7.4 %down_pieces.3 = (bf16[2,2,192,768]{3,2,1,0:T(8,128)(2,1)}, bf16[2,2,192,768]{3,2,1,0:T(8,128)(2,1)}) custom-call(s32[4]{0:T(128)} %pad_add_fusion.bits_ref, bf16[1024,1536]{1,0:T(8,128)(2,1)} %get-tuple-element.273.act_ref, bf16[1024,768]{1,0:T(8,128)(2,1)} %get-tuple-element.260.grad_ref), custom_call_target="tpu_custom_call" | custom-call | flops 1000000 | bytes 100000 | tf_op jit(solution)/shard_map/down_pieces/pallas_call | solution.py:630
  170.6 11.1 %attend_back.2.grads_ref.other_ref = bf16[3,1024,384]{2,1,0:T(8,128)(2,1)} custom-call(bf16[1024,384]{1,0:T(8,128)(2,1)} %get-tuple-element.275.q_ref, bf16[1024,384]{1,0:T(8,128)(2,1)} %get-tuple-element.276.k_ref, bf16[1024,384]{1,0:T(8,128)(2,1)} %get-tuple-element.222.v_ref, bf16[1024,384]{1,0:T(8,128)(2,1)} %get-tuple-element.278.other_context_ref.context_ref, ...), custom_call_target="tpu_custom_call" | custom-call | flops 1000000 | bytes 100000 | tf_op jit(solution)/shard_map/attend_back/pallas_call | solution.py:110
  182.8 1.9 collective-permute-done.13
  184.7 2.3 fusion
  187.0 9.0 %collective-permute-done.11 = bf16[2,2,192,768]{3,2,1,0:T(8,128)(2,1)} collective-permute-done((bf16[2,2,192,768]{3,2,1,0:T(8,128)(2,1)S(1)}, bf16[2,2,192,768]{3,2,1,0:T(8,128)(2,1)}, u32[]{:S(2)}, u32[]{:S(2)}) %collective-permute-start.11) | collective-permute-done | bytes 1179680 | tf_op jit(solution)/shard_map/ppermute | solution.py:27
  196.0 2.3 fusion.3
  198.2 8.4 %heads_pieces.2 = (bf16[4,4,96,384]{3,2,1,0:T(8,128)(2,1)}, bf16[4,4,96,384]{3,2,1,0:T(8,128)(2,1)}) custom-call(s32[4]{0:T(128)} %pad_add_fusion.bits_ref, bf16[2048,768]{1,0:T(8,128)(2,1)} %x_ref.8, bf16[3,1024,384]{2,1,0:T(8,128)(2,1)} %attend_back.2.grads_ref.other_ref, bf16[1024,384]{1,0:T(8,128)(2,1)} %get-tuple-element.278.other_context_ref.context_ref, ...), custom_call_target="tpu_custom_call" | custom-call | flops 1000000 | bytes 100000 | tf_op jit(solution)/shard_map/heads_pieces/pallas_call | solution.py:720
  212.4 1.6 add_convert_fusion
  214.7 11.2 %attend_back.3.grads_ref.own_ref = bf16[3,1024,384]{2,1,0:T(8,128)(2,1)} custom-call(bf16[1024,384]{1,0:T(8,128)(2,1)} %get-tuple-element.301.q_ref, bf16[1024,384]{1,0:T(8,128)(2,1)} %get-tuple-element.302.k_ref, bf16[1024,384]{1,0:T(8,128)(2,1)} %get-tuple-element.210.v_ref, bf16[1024,384]{1,0:T(8,128)(2,1)} %get-tuple-element.304.own_context_ref.context_ref, ...), custom_call_target="tpu_custom_call" | custom-call | flops 1000000 | bytes 100000 | tf_op jit(solution)/shard_map/attend_back/pallas_call | solution.py:110
  225.9 1.9 fusion.13
  229.3 8.2 %collective-permute-done.16 = bf16[2,192,768]{2,1,0:T(8,128)(2,1)} collective-permute-done((bf16[2,192,768]{2,1,0:T(8,128)(2,1)}, bf16[2,192,768]{2,1,0:T(8,128)(2,1)}, u32[]{:S(2)}, u32[]{:S(2)}) %collective-permute-start.16) | collective-permute-done | bytes 589856 | tf_op jit(solution)/shard_map/ppermute | solution.py:23
  237.5 2.1 fusion.12
  239.6 8.3 %heads_pieces.3 = (bf16[4,4,96,384]{3,2,1,0:T(8,128)(2,1)}, bf16[4,4,96,384]{3,2,1,0:T(8,128)(2,1)}) custom-call(s32[4]{0:T(128)} %pad_add_fusion.bits_ref, bf16[2048,768]{1,0:T(8,128)(2,1)} %x_ref.8, bf16[3,1024,384]{2,1,0:T(8,128)(2,1)} %attend_back.3.grads_ref.own_ref, bf16[1024,384]{1,0:T(8,128)(2,1)} %get-tuple-element.304.own_context_ref.context_ref, ...), custom_call_target="tpu_custom_call" | custom-call | flops 1000000 | bytes 100000 | tf_op jit(solution)/shard_map/heads_pieces/pallas_call | solution.py:720
  247.9 1.6 collective-permute-start.19
  250.0 2.0 fusion.11
  252.1 2.6 collective-permute-start.28
  254.6 6.8 %collective-permute-done.19 = bf16[192,768]{1,0:T(8,128)(2,1)S(1)} collective-permute-done((bf16[192,768]{1,0:T(8,128)(2,1)}, bf16[192,768]{1,0:T(8,128)(2,1)S(1)}, u32[]{:S(2)}, u32[]{:S(2)}) %collective-permute-start.19) | collective-permute-done | bytes 294944 | tf_op jit(solution)/shard_map/ppermute | solution.py:23
  261.5 2.1 fusion.9
  263.6 11.9 %project_back.1 = bf16[1024,768]{1,0:T(8,128)(2,1)} custom-call(s32[4]{0:T(128)} %pad_add_fusion.bits_ref, bf16[3,1024,384]{2,1,0:T(8,128)(2,1)} %attend_back.3.grads_ref.own_ref, bf16[3,1024,384]{2,1,0:T(8,128)(2,1)} %attend_back.2.grads_ref.other_ref, bf16[1024,768]{1,0:T(8,128)(2,1)} %get-tuple-element.292.attended_ref.grad_ref, ...), custom_call_target="tpu_custom_call" | custom-call | flops 1000000 | bytes 100000 | tf_op jit(solution)/shard_map/project_back/pallas_call | solution.py:318
  279.9 1.6 collective-permute-start.24
  285.0 2.4 collective-permute-start.33
  287.4 9.6 %collective-permute-done.27 = bf16[192,768]{1,0:T(8,128)(2,1)S(1)} collective-permute-done((bf16[192,768]{1,0:T(8,128)(2,1)S(1)}, bf16[192,768]{1,0:T(8,128)(2,1)S(1)}, u32[]{:S(2)}, u32[]{:S(2)}) %collective-permute-start.27) | collective-permute-done | bytes 294944 | tf_op jit(solution)/shard_map/ppermute | solution.py:23
  298.5 2.1 collective-permute-start.29
  303.0 11.0 %collective-permute-done.30 = f32[6912]{0:T(1024)S(1)} collective-permute-done((f32[6912]{0:T(1024)S(1)}, f32[6912]{0:T(1024)S(1)}, u32[]{:S(2)}, u32[]{:S(2)}) %collective-permute-start.30) | collective-permute-done | bytes 27680 | tf_op jit(solution)/shard_map/ppermute | solution.py:23
  318.6 5.3 %collective-permute-done.42.refs_2_ = bf16[192,768]{1,0:T(8,128)(2,1)S(1)} collective-permute-done((bf16[192,768]{1,0:T(8,128)(2,1)S(1)}, bf16[192,768]{1,0:T(8,128)(2,1)S(1)}, u32[]{:S(2)}, u32[]{:S(2)}) %collective-permute-start.42) | collective-permute-done | bytes 294944 | tf_op jit(solution)/shard_map/ppermute | solution.py:23
  325.0 3.6 collective-permute-done.43.refs_3_
  331.8 4.0 %widen.3 = f32[768,1536]{1,0:T(8,128)} custom-call(s32[4]{0:T(128)} %pad_add_fusion.bits_ref, bf16[384,384]{1,0:T(8,128)(2,1)} %copy-done.7, bf16[384,384]{1,0:T(8,128)(2,1)} %copy-done.25, bf16[384,384]{1,0:T(8,128)(2,1)} %copy-done.28, bf16[384,384]{1,0:T(8,128)(2,1)} %copy-done.29, bf16[384,384]{1,0:T(8,128)(2,1)} %copy-done.30, ...), custom_call_target="tpu_custom_call" | custom-call | flops 1000000 | bytes 100000 | tf_op jit(solution)/shard_map/widen/pallas_call | solution.py:825
  335.8 6.0 %collective-permute-done.32 = f32[6912]{0:T(1024)S(1)} collective-permute-done((f32[6912]{0:T(1024)}, f32[6912]{0:T(1024)S(1)}, u32[]{:S(2)}, u32[]{:S(2)}) %collective-permute-start.32) | collective-permute-done | bytes 27680 | tf_op jit(solution)/shard_map/ppermute | solution.py:23
  345.7 4.0 %widen.4 = f32[1536,768]{1,0:T(8,128)} custom-call(s32[4]{0:T(128)} %pad_add_fusion.bits_ref, bf16[192,768]{1,0:T(8,128)(2,1)} %copy-done.6, bf16[192,768]{1,0:T(8,128)(2,1)} %copy-done.24, bf16[192,768]{1,0:T(8,128)(2,1)} %copy-done.26, bf16[192,768]{1,0:T(8,128)(2,1)} %copy-done.27, bf16[192,768]{1,0:T(8,128)(2,1)} %copy-done.31, ...), custom_call_target="tpu_custom_call" | custom-call | flops 1000000 | bytes 100000 | tf_op jit(solution)/shard_map/widen/pallas_call | solution.py:825
  349.7 3.4 collective-permute-done.40.refs_1_
  354.1 7.6 %collective-permute-done.49.refs_3_ = bf16[4,96,384]{2,1,0:T(8,128)(2,1)S(1)} collective-permute-done((bf16[4,96,384]{2,1,0:T(8,128)(2,1)S(1)}, bf16[4,96,384]{2,1,0:T(8,128)(2,1)S(1)}, u32[]{:S(2)}, u32[]{:S(2)}) %collective-permute-start.49) | collective-permute-done | bytes 294944 | tf_op jit(solution)/shard_map/ppermute | solution.py:23
  365.7 4.0 %widen.5 = (f32[3,768,384]{2,1,0:T(8,128)}, f32[384,768]{1,0:T(8,128)}) custom-call(s32[4]{0:T(128)} %pad_add_fusion.bits_ref, bf16[4,96,384]{2,1,0:T(8,128)(2,1)} %copy-done.12, bf16[4,96,384]{2,1,0:T(8,128)(2,1)} %copy-done.37, bf16[4,96,384]{2,1,0:T(8,128)(2,1)} %copy-done.38, bf16[4,96,384]{2,1,0:T(8,128)(2,1)} %copy-done.39, ...), custom_call_target="tpu_custom_call" | custom-call | flops 1000000 | bytes 100000 | tf_op jit(solution)/shard_map/widen/pallas_call | solution.py:825
  (235 shorter events, 52.4 us)
Async XLA Ops:
  4.8 16.5 %collective-permute-start.1 = (bf16[4,192,384]{2,1,0:T(8,128)(2,1)}, bf16[4,192,384]{2,1,0:T(8,128)(2,1)S(1)}, u32[]{:S(2)}, u32[]{:S(2)}) collective-permute-start(bf16[4,192,384]{2,1,0:T(8,128)(2,1)} %get-tuple-element.204), channel_id=1, source_target_pairs={{0,1},{1,0},{2,3},{3,2},{4,5},{5,4},{6,7},{7,6},{8,9},{9,8},{10,11... | collective-permute-start | bytes 1769480 | tf_op jit(solution)/shard_map/ppermute | solution.py:27
  21.3 14.7 %collective-permute-start.2 = (bf16[4,192,384]{2,1,0:T(8,128)(2,1)S(1)}, bf16[4,192,384]{2,1,0:T(8,128)(2,1)S(1)}, u32[]{:S(2)}, u32[]{:S(2)}) collective-permute-start(bf16[4,192,384]{2,1,0:T(8,128)(2,1)S(1)} %collective-permute-done.1.refs_0_), channel_id=1, source_target_pairs={{0,4},{2,6},{4,0},{6,2},{8,12},{10,14},{12,8},{14,10},{16,20},{18,... | collective-permute-start | bytes 1769480 | tf_op jit(solution)/shard_map/ppermute | solution.py:23
  23.8 36.4 %collective-permute-start.5 = (bf16[768,768]{1,0:T(8,128)(2,1)}, bf16[768,768]{1,0:T(8,128)(2,1)S(1)}, u32[]{:S(2)}, u32[]{:S(2)}) collective-permute-start(bf16[768,768]{1,0:T(8,128)(2,1)} %get-tuple-element.234), channel_id=1, source_target_pairs={{0,1},{1,0},{2,3},{3,2},{4,5},{5,4},{6,7},{7,6},{8,9},{9,8},{10,11... | collective-permute-start | bytes 3538952 | tf_op jit(solution)/shard_map/ppermute | solution.py:27
  36.0 14.8 %collective-permute-start.3 = (bf16[4,192,384]{2,1,0:T(8,128)(2,1)S(1)}, bf16[4,192,384]{2,1,0:T(8,128)(2,1)S(1)}, u32[]{:S(2)}, u32[]{:S(2)}) collective-permute-start(bf16[4,192,384]{2,1,0:T(8,128)(2,1)S(1)} %collective-permute-done.1.refs_0_), channel_id=1, source_target_pairs={{0,2},{2,0},{4,6},{6,4},{8,10},{10,8},{12,14},{14,12},{16,18},{18,... | collective-permute-start | bytes 1769480 | tf_op jit(solution)/shard_map/ppermute | solution.py:23
  36.0 15.4 %collective-permute-start.4 = (bf16[4,192,384]{2,1,0:T(8,128)(2,1)S(1)}, bf16[4,192,384]{2,1,0:T(8,128)(2,1)S(1)}, u32[]{:S(2)}, u32[]{:S(2)}) collective-permute-start(bf16[4,192,384]{2,1,0:T(8,128)(2,1)S(1)} %collective-permute-done.2.refs_1_), channel_id=1, source_target_pairs={{0,2},{2,0},{4,6},{6,4},{8,10},{10,8},{12,14},{14,12},{16,18},{18,... | collective-permute-start | bytes 1769480 | tf_op jit(solution)/shard_map/ppermute | solution.py:23
  36.5 14.3 %collective-permute-start = (f32[6,384]{1,0:T(8,128)S(1)}, f32[6,384]{1,0:T(8,128)S(1)}, u32[]{:S(2)}, u32[]{:S(2)}) collective-permute-start(f32[6,384]{1,0:T(8,128)S(1)} %copy-done.44), channel_id=1, source_target_pairs={{0,1},{1,0},{2,3},{3,2},{4,5},{5,4},{6,7},{7,6},{8,9},{9,8},{10,11... | collective-permute-start | bytes 27656 | tf_op jit(solution)/shard_map/ppermute | solution.py:27
  60.2 31.5 %collective-permute-start.6 = (bf16[768,768]{1,0:T(8,128)(2,1)S(1)}, bf16[768,768]{1,0:T(8,128)(2,1)S(1)}, u32[]{:S(2)}, u32[]{:S(2)}) collective-permute-start(bf16[768,768]{1,0:T(8,128)(2,1)S(1)} %collective-permute-done.5.refs_4_), channel_id=1, source_target_pairs={{0,4},{2,6},{4,0},{6,2},{8,12},{10,14},{12,8},{14,10},{16,20},{18,... | collective-permute-start | bytes 3538952 | tf_op jit(solution)/shard_map/ppermute | solution.py:23
  60.9 31.4 %collective-permute-start.7 = (bf16[768,768]{1,0:T(8,128)(2,1)S(1)}, bf16[768,768]{1,0:T(8,128)(2,1)S(1)}, u32[]{:S(2)}, u32[]{:S(2)}) collective-permute-start(bf16[768,768]{1,0:T(8,128)(2,1)S(1)} %collective-permute-done.5.refs_4_), channel_id=1, source_target_pairs={{0,2},{2,0},{4,6},{6,4},{8,10},{10,8},{12,14},{14,12},{16,18},{18,... | collective-permute-start | bytes 3538952 | tf_op jit(solution)/shard_map/ppermute | solution.py:23
  142.3 7.8 %collective-permute-start.10 = (bf16[2,2,192,768]{3,2,1,0:T(8,128)(2,1)}, bf16[2,2,192,768]{3,2,1,0:T(8,128)(2,1)S(1)}, u32[]{:S(2)}, u32[]{:S(2)}) collective-permute-start(bf16[2,2,192,768]{3,2,1,0:T(8,128)(2,1)} %get-tuple-element.261), channel_id=1, source_target_pairs={{0,2},{2,0},{4,6},{6,4},{8,10},{10,8},{12,14},{14,12},{16,18},{18,... | collective-permute-start | bytes 3538952 | tf_op jit(solution)/shard_map/ppermute | solution.py:23
  149.9 8.1 %collective-permute-start.9 = (bf16[2,2,384,384]{3,2,1,0:T(8,128)(2,1)}, bf16[2,2,384,384]{3,2,1,0:T(8,128)(2,1)}, u32[]{:S(2)}, u32[]{:S(2)}) collective-permute-start(bf16[2,2,384,384]{3,2,1,0:T(8,128)(2,1)} %get-tuple-element.264), channel_id=1, source_target_pairs={{0,2},{2,0},{4,6},{6,4},{8,10},{10,8},{12,14},{14,12},{16,18},{18,... | collective-permute-start | bytes 3538952 | tf_op jit(solution)/shard_map/ppermute | solution.py:23
  157.7 24.0 %collective-permute-start.14 = (bf16[2,2,384,384]{3,2,1,0:T(8,128)(2,1)}, bf16[2,2,384,384]{3,2,1,0:T(8,128)(2,1)S(1)}, u32[]{:S(2)}, u32[]{:S(2)}) collective-permute-start(bf16[2,2,384,384]{3,2,1,0:T(8,128)(2,1)} %get-tuple-element.270), channel_id=1, source_target_pairs={{0,2},{2,0},{4,6},{6,4},{8,10},{10,8},{12,14},{14,12},{16,18},{18,... | collective-permute-start | bytes 3538952 | tf_op jit(solution)/shard_map/ppermute | solution.py:23
  167.5 19.5 %collective-permute-start.12 = (bf16[2,2,192,768]{3,2,1,0:T(8,128)(2,1)}, bf16[2,2,192,768]{3,2,1,0:T(8,128)(2,1)}, u32[]{:S(2)}, u32[]{:S(2)}) collective-permute-start(bf16[2,2,192,768]{3,2,1,0:T(8,128)(2,1)} %get-tuple-element.274), channel_id=1, source_target_pairs={{0,2},{2,0},{4,6},{6,4},{8,10},{10,8},{12,14},{14,12},{16,18},{18,... | collective-permute-start | bytes 3538952 | tf_op jit(solution)/shard_map/ppermute | solution.py:23
  167.7 28.3 %collective-permute-start.11 = (bf16[2,2,192,768]{3,2,1,0:T(8,128)(2,1)S(1)}, bf16[2,2,192,768]{3,2,1,0:T(8,128)(2,1)}, u32[]{:S(2)}, u32[]{:S(2)}) collective-permute-start(bf16[2,2,192,768]{3,2,1,0:T(8,128)(2,1)S(1)} %add_convert_fusion.1), channel_id=1, source_target_pairs={{0,1},{1,0},{2,3},{3,2},{4,5},{5,4},{6,7},{7,6},{8,9},{9,8},{10,11... | collective-permute-start | bytes 3538952 | tf_op jit(solution)/shard_map/ppermute | solution.py:27
  169.1 15.6 %collective-permute-start.13 = (bf16[2,384,384]{2,1,0:T(8,128)(2,1)}, bf16[2,384,384]{2,1,0:T(8,128)(2,1)}, u32[]{:S(2)}, u32[]{:S(2)}) collective-permute-start(bf16[2,384,384]{2,1,0:T(8,128)(2,1)} %fusion.1), channel_id=1, source_target_pairs={{0,4},{2,6},{4,0},{6,2},{8,12},{10,14},{12,8},{14,10},{16,20},{18,... | collective-permute-start | bytes 1769480 | tf_op jit(solution)/shard_map/ppermute | solution.py:23
  207.6 18.3 %collective-permute-start.18 = (bf16[2,384,384]{2,1,0:T(8,128)(2,1)}, bf16[2,384,384]{2,1,0:T(8,128)(2,1)}, u32[]{:S(2)}, u32[]{:S(2)}) collective-permute-start(bf16[2,384,384]{2,1,0:T(8,128)(2,1)} %fusion), channel_id=1, source_target_pairs={{0,1},{1,0},{2,3},{3,2},{4,5},{5,4},{6,7},{7,6},{8,9},{9,8},{10,11... | collective-permute-start | bytes 1769480 | tf_op jit(solution)/shard_map/ppermute | solution.py:27
  209.1 16.8 %collective-permute-start.17 = (bf16[2,384,384]{2,1,0:T(8,128)(2,1)}, bf16[2,384,384]{2,1,0:T(8,128)(2,1)}, u32[]{:S(2)}, u32[]{:S(2)}) collective-permute-start(bf16[2,384,384]{2,1,0:T(8,128)(2,1)} %fusion.2), channel_id=1, source_target_pairs={{0,4},{2,6},{4,0},{6,2},{8,12},{10,14},{12,8},{14,10},{16,20},{18,... | collective-permute-start | bytes 1769480 | tf_op jit(solution)/shard_map/ppermute | solution.py:23
  210.6 26.9 %collective-permute-start.16 = (bf16[2,192,768]{2,1,0:T(8,128)(2,1)}, bf16[2,192,768]{2,1,0:T(8,128)(2,1)}, u32[]{:S(2)}, u32[]{:S(2)}) collective-permute-start(bf16[2,192,768]{2,1,0:T(8,128)(2,1)} %fusion.3), channel_id=1, source_target_pairs={{0,4},{2,6},{4,0},{6,2},{8,12},{10,14},{12,8},{14,10},{16,20},{18,... | collective-permute-start | bytes 1769480 | tf_op jit(solution)/shard_map/ppermute | solution.py:23
  214.0 64.3 %collective-permute-start.21 = (bf16[2,2,4,96,384]{4,3,2,1,0:T(8,128)(2,1)S(1)}, bf16[2,2,4,96,384]{4,3,2,1,0:T(8,128)(2,1)}, u32[]{:S(2)}, u32[]{:S(2)}) collective-permute-start(bf16[2,2,4,96,384]{4,3,2,1,0:T(8,128)(2,1)S(1)} %add_convert_fusion), channel_id=1, source_target_pairs={{0,1},{1,0},{2,3},{3,2},{4,5},{5,4},{6,7},{7,6},{8,9},{9,8},{10,11... | collective-permute-start | bytes 3538952 | tf_op jit(solution)/shard_map/ppermute | solution.py:27
  227.8 22.2 %collective-permute-start.20 = (bf16[384,384]{1,0:T(8,128)(2,1)}, bf16[384,384]{1,0:T(8,128)(2,1)}, u32[]{:S(2)}, u32[]{:S(2)}) collective-permute-start(bf16[384,384]{1,0:T(8,128)(2,1)} %fusion.13), channel_id=1, source_target_pairs={{0,8},{2,10},{4,12},{6,14},{8,0},{10,2},{12,4},{14,6},{16,24},{18,... | collective-permute-start | bytes 884744 | tf_op jit(solution)/shard_map/ppermute | solution.py:23
  247.9 30.4 %collective-permute-start.22 = (bf16[2,2,4,96,384]{4,3,2,1,0:T(8,128)(2,1)}, bf16[2,2,4,96,384]{4,3,2,1,0:T(8,128)(2,1)}, u32[]{:S(2)}, u32[]{:S(2)}) collective-permute-start(bf16[2,2,4,96,384]{4,3,2,1,0:T(8,128)(2,1)} %bitcast.70), channel_id=1, source_target_pairs={{0,2},{2,0},{4,6},{6,4},{8,10},{10,8},{12,14},{14,12},{16,18},{18,... | collective-permute-start | bytes 3538952 | tf_op jit(solution)/shard_map/ppermute | solution.py:23
  247.9 13.6 %collective-permute-start.19 = (bf16[192,768]{1,0:T(8,128)(2,1)}, bf16[192,768]{1,0:T(8,128)(2,1)S(1)}, u32[]{:S(2)}, u32[]{:S(2)}) collective-permute-start(bf16[192,768]{1,0:T(8,128)(2,1)} %fusion.12), channel_id=1, source_target_pairs={{0,8},{2,10},{4,12},{6,14},{8,0},{10,2},{12,4},{14,6},{16,24},{18,... | collective-permute-start | bytes 884744 | tf_op jit(solution)/shard_map/ppermute | solution.py:23
  249.5 26.0 %collective-permute-start.23 = (f32[6912]{0:T(1024)}, f32[6912]{0:T(1024)}, u32[]{:S(2)}, u32[]{:S(2)}) collective-permute-start(f32[6912]{0:T(1024)} %pad_maximum_fusion), channel_id=1, source_target_pairs={{0,1},{1,0},{2,3},{3,2},{4,5},{5,4},{6,7},{7,6},{8,9},{9,8},{10,11... | collective-permute-start | bytes 82952 | tf_op jit(solution)/shard_map/ppermute | solution.py:27
  252.1 31.8 %collective-permute-start.28 = (bf16[384,384]{1,0:T(8,128)(2,1)}, bf16[384,384]{1,0:T(8,128)(2,1)}, u32[]{:S(2)}, u32[]{:S(2)}) collective-permute-start(bf16[384,384]{1,0:T(8,128)(2,1)} %fusion.11), channel_id=1, source_target_pairs={{0,16},{2,18},{4,20},{6,22},{8,24},{10,26},{12,28},{14,30},{16,0},... | collective-permute-start | bytes 884744 | tf_op jit(solution)/shard_map/ppermute | solution.py:23
  279.9 17.4 %collective-permute-start.24 = (bf16[2,4,96,384]{3,2,1,0:T(8,128)(2,1)S(1)}, bf16[2,4,96,384]{3,2,1,0:T(8,128)(2,1)S(1)}, u32[]{:S(2)}, u32[]{:S(2)}) collective-permute-start(bf16[2,4,96,384]{3,2,1,0:T(8,128)(2,1)S(1)} %fusion.4), channel_id=1, source_target_pairs={{0,4},{2,6},{4,0},{6,2},{8,12},{10,14},{12,8},{14,10},{16,20},{18,... | collective-permute-start | bytes 1769480 | tf_op jit(solution)/shard_map/ppermute | solution.py:23
  281.4 15.6 %collective-permute-start.27 = (bf16[192,768]{1,0:T(8,128)(2,1)S(1)}, bf16[192,768]{1,0:T(8,128)(2,1)S(1)}, u32[]{:S(2)}, u32[]{:S(2)}) collective-permute-start(bf16[192,768]{1,0:T(8,128)(2,1)S(1)} %copy-done.15), channel_id=1, source_target_pairs={{0,16},{2,18},{4,20},{6,22},{8,24},{10,26},{12,28},{14,30},{16,0},... | collective-permute-start | bytes 884744 | tf_op jit(solution)/shard_map/ppermute | solution.py:23
  283.3 13.9 %collective-permute-start.26 = (f32[6912]{0:T(1024)S(1)}, f32[6912]{0:T(1024)S(1)}, u32[]{:S(2)}, u32[]{:S(2)}) collective-permute-start(f32[6912]{0:T(1024)S(1)} %add.178), channel_id=1, source_target_pairs={{0,4},{2,6},{4,0},{6,2},{8,12},{10,14},{12,8},{14,10},{16,20},{18,... | collective-permute-start | bytes 82952 | tf_op jit(solution)/shard_map/ppermute | solution.py:23
  285.0 16.5 %collective-permute-start.33 = (bf16[384,384]{1,0:T(8,128)(2,1)S(1)}, bf16[384,384]{1,0:T(8,128)(2,1)S(1)}, u32[]{:S(2)}, u32[]{:S(2)}) collective-permute-start(bf16[384,384]{1,0:T(8,128)(2,1)S(1)} %add_convert_fusion.8.refs_0_), channel_id=1, source_target_pairs={{0,8},{2,10},{4,12},{6,14},{8,0},{10,2},{12,4},{14,6},{16,24},{18,... | collective-permute-start | bytes 884744 | tf_op jit(solution)/shard_map/ppermute | solution.py:23
  297.1 18.3 %collective-permute-start.41 = (bf16[192,768]{1,0:T(8,128)(2,1)S(1)}, bf16[192,768]{1,0:T(8,128)(2,1)S(1)}, u32[]{:S(2)}, u32[]{:S(2)}) collective-permute-start(bf16[192,768]{1,0:T(8,128)(2,1)S(1)} %add_convert_fusion.7.refs_0_), channel_id=1, source_target_pairs={{0,8},{2,10},{4,12},{6,14},{8,0},{10,2},{12,4},{14,6},{16,24},{18,... | collective-permute-start | bytes 884744 | tf_op jit(solution)/shard_map/ppermute | solution.py:23
  298.5 17.7 %collective-permute-start.29 = (bf16[4,96,384]{2,1,0:T(8,128)(2,1)S(1)}, bf16[4,96,384]{2,1,0:T(8,128)(2,1)S(1)}, u32[]{:S(2)}, u32[]{:S(2)}) collective-permute-start(bf16[4,96,384]{2,1,0:T(8,128)(2,1)S(1)} %fusion.7), channel_id=1, source_target_pairs={{0,8},{2,10},{4,12},{6,14},{8,0},{10,2},{12,4},{14,6},{16,24},{18,... | collective-permute-start | bytes 884744 | tf_op jit(solution)/shard_map/ppermute | solution.py:23
  300.5 13.4 %collective-permute-start.30 = (f32[6912]{0:T(1024)S(1)}, f32[6912]{0:T(1024)S(1)}, u32[]{:S(2)}, u32[]{:S(2)}) collective-permute-start(f32[6912]{0:T(1024)S(1)} %add.181), channel_id=1, source_target_pairs={{0,8},{2,10},{4,12},{6,14},{8,0},{10,2},{12,4},{14,6},{16,24},{18,... | collective-permute-start | bytes 82952 | tf_op jit(solution)/shard_map/ppermute | solution.py:23
  300.6 17.4 %collective-permute-start.34 = (bf16[384,384]{1,0:T(8,128)(2,1)S(1)}, bf16[384,384]{1,0:T(8,128)(2,1)S(1)}, u32[]{:S(2)}, u32[]{:S(2)}) collective-permute-start(bf16[384,384]{1,0:T(8,128)(2,1)S(1)} %add_convert_fusion.8.refs_0_), channel_id=1, source_target_pairs={{0,4},{2,6},{4,0},{6,2},{8,12},{10,14},{12,8},{14,10},{16,20},{18,... | collective-permute-start | bytes 884744 | tf_op jit(solution)/shard_map/ppermute | solution.py:23
  301.5 16.8 %collective-permute-start.35 = (bf16[384,384]{1,0:T(8,128)(2,1)S(1)}, bf16[384,384]{1,0:T(8,128)(2,1)S(1)}, u32[]{:S(2)}, u32[]{:S(2)}) collective-permute-start(bf16[384,384]{1,0:T(8,128)(2,1)S(1)} %collective-permute-done.33.refs_1_), channel_id=1, source_target_pairs={{0,4},{2,6},{4,0},{6,2},{8,12},{10,14},{12,8},{14,10},{16,20},{18,... | collective-permute-start | bytes 884744 | tf_op jit(solution)/shard_map/ppermute | solution.py:23
  314.0 9.9 %collective-permute-start.42 = (bf16[192,768]{1,0:T(8,128)(2,1)S(1)}, bf16[192,768]{1,0:T(8,128)(2,1)S(1)}, u32[]{:S(2)}, u32[]{:S(2)}) collective-permute-start(bf16[192,768]{1,0:T(8,128)(2,1)S(1)} %add_convert_fusion.7.refs_0_), channel_id=1, source_target_pairs={{0,4},{2,6},{4,0},{6,2},{8,12},{10,14},{12,8},{14,10},{16,20},{18,... | collective-permute-start | bytes 884744 | tf_op jit(solution)/shard_map/ppermute | solution.py:23
  315.5 8.5 %collective-permute-start.36 = (bf16[384,384]{1,0:T(8,128)(2,1)S(1)}, bf16[384,384]{1,0:T(8,128)(2,1)S(1)}, u32[]{:S(2)}, u32[]{:S(2)}) collective-permute-start(bf16[384,384]{1,0:T(8,128)(2,1)S(1)} %add_convert_fusion.8.refs_0_), channel_id=1, source_target_pairs={{0,2},{2,0},{4,6},{6,4},{8,10},{10,8},{12,14},{14,12},{16,18},{18,... | collective-permute-start | bytes 884744 | tf_op jit(solution)/shard_map/ppermute | solution.py:23
  316.2 12.4 %collective-permute-start.43 = (bf16[192,768]{1,0:T(8,128)(2,1)S(1)}, bf16[192,768]{1,0:T(8,128)(2,1)S(1)}, u32[]{:S(2)}, u32[]{:S(2)}) collective-permute-start(bf16[192,768]{1,0:T(8,128)(2,1)S(1)} %collective-permute-done.41.refs_1_), channel_id=1, source_target_pairs={{0,4},{2,6},{4,0},{6,2},{8,12},{10,14},{12,8},{14,10},{16,20},{18,... | collective-permute-start | bytes 884744 | tf_op jit(solution)/shard_map/ppermute | solution.py:23
  318.0 11.7 %collective-permute-start.37 = (bf16[384,384]{1,0:T(8,128)(2,1)S(1)}, bf16[384,384]{1,0:T(8,128)(2,1)S(1)}, u32[]{:S(2)}, u32[]{:S(2)}) collective-permute-start(bf16[384,384]{1,0:T(8,128)(2,1)S(1)} %collective-permute-done.33.refs_1_), channel_id=1, source_target_pairs={{0,2},{2,0},{4,6},{6,4},{8,10},{10,8},{12,14},{14,12},{16,18},{18,... | collective-permute-start | bytes 884744 | tf_op jit(solution)/shard_map/ppermute | solution.py:23
  318.2 11.5 %collective-permute-start.38 = (bf16[384,384]{1,0:T(8,128)(2,1)S(1)}, bf16[384,384]{1,0:T(8,128)(2,1)S(1)}, u32[]{:S(2)}, u32[]{:S(2)}) collective-permute-start(bf16[384,384]{1,0:T(8,128)(2,1)S(1)} %collective-permute-done.34.refs_2_), channel_id=1, source_target_pairs={{0,2},{2,0},{4,6},{6,4},{8,10},{10,8},{12,14},{14,12},{16,18},{18,... | collective-permute-start | bytes 884744 | tf_op jit(solution)/shard_map/ppermute | solution.py:23
  323.9 6.4 %collective-permute-start.39 = (bf16[384,384]{1,0:T(8,128)(2,1)S(1)}, bf16[384,384]{1,0:T(8,128)(2,1)S(1)}, u32[]{:S(2)}, u32[]{:S(2)}) collective-permute-start(bf16[384,384]{1,0:T(8,128)(2,1)S(1)} %collective-permute-done.35.refs_3_), channel_id=1, source_target_pairs={{0,2},{2,0},{4,6},{6,4},{8,10},{10,8},{12,14},{14,12},{16,18},{18,... | collective-permute-start | bytes 884744 | tf_op jit(solution)/shard_map/ppermute | solution.py:23
  323.9 18.6 %collective-permute-start.31 = (bf16[4,96,384]{2,1,0:T(8,128)(2,1)S(1)}, bf16[4,96,384]{2,1,0:T(8,128)(2,1)}, u32[]{:S(2)}, u32[]{:S(2)}) collective-permute-start(bf16[4,96,384]{2,1,0:T(8,128)(2,1)S(1)} %fusion.6), channel_id=1, source_target_pairs={{0,16},{2,18},{4,20},{6,22},{8,24},{10,26},{12,28},{14,30},{16,0},... | collective-permute-start | bytes 884744 | tf_op jit(solution)/shard_map/ppermute | solution.py:23
  328.5 13.3 %collective-permute-start.32 = (f32[6912]{0:T(1024)}, f32[6912]{0:T(1024)S(1)}, u32[]{:S(2)}, u32[]{:S(2)}) collective-permute-start(f32[6912]{0:T(1024)} %add.186), channel_id=1, source_target_pairs={{0,16},{2,18},{4,20},{6,22},{8,24},{10,26},{12,28},{14,30},{16,0},... | collective-permute-start | bytes 82952 | tf_op jit(solution)/shard_map/ppermute | solution.py:23
  329.7 14.0 %collective-permute-start.44 = (bf16[192,768]{1,0:T(8,128)(2,1)S(1)}, bf16[192,768]{1,0:T(8,128)(2,1)S(1)}, u32[]{:S(2)}, u32[]{:S(2)}) collective-permute-start(bf16[192,768]{1,0:T(8,128)(2,1)S(1)} %add_convert_fusion.7.refs_0_), channel_id=1, source_target_pairs={{0,2},{2,0},{4,6},{6,4},{8,10},{10,8},{12,14},{14,12},{16,18},{18,... | collective-permute-start | bytes 884744 | tf_op jit(solution)/shard_map/ppermute | solution.py:23
  329.8 14.5 %collective-permute-start.45 = (bf16[192,768]{1,0:T(8,128)(2,1)S(1)}, bf16[192,768]{1,0:T(8,128)(2,1)S(1)}, u32[]{:S(2)}, u32[]{:S(2)}) collective-permute-start(bf16[192,768]{1,0:T(8,128)(2,1)S(1)} %collective-permute-done.41.refs_1_), channel_id=1, source_target_pairs={{0,2},{2,0},{4,6},{6,4},{8,10},{10,8},{12,14},{14,12},{16,18},{18,... | collective-permute-start | bytes 884744 | tf_op jit(solution)/shard_map/ppermute | solution.py:23
  331.3 13.0 %collective-permute-start.46 = (bf16[192,768]{1,0:T(8,128)(2,1)S(1)}, bf16[192,768]{1,0:T(8,128)(2,1)}, u32[]{:S(2)}, u32[]{:S(2)}) collective-permute-start(bf16[192,768]{1,0:T(8,128)(2,1)S(1)} %collective-permute-done.42.refs_2_), channel_id=1, source_target_pairs={{0,2},{2,0},{4,6},{6,4},{8,10},{10,8},{12,14},{14,12},{16,18},{18,... | collective-permute-start | bytes 884744 | tf_op jit(solution)/shard_map/ppermute | solution.py:23
  343.6 9.5 %collective-permute-start.40 = (bf16[4,96,384]{2,1,0:T(8,128)(2,1)S(1)}, bf16[4,96,384]{2,1,0:T(8,128)(2,1)S(1)}, u32[]{:S(2)}, u32[]{:S(2)}) collective-permute-start(bf16[4,96,384]{2,1,0:T(8,128)(2,1)S(1)} %add_convert_fusion.6.refs_0_), channel_id=1, source_target_pairs={{0,8},{2,10},{4,12},{6,14},{8,0},{10,2},{12,4},{14,6},{16,24},{18,... | collective-permute-start | bytes 884744 | tf_op jit(solution)/shard_map/ppermute | solution.py:23
  343.7 10.4 %collective-permute-start.48 = (bf16[4,96,384]{2,1,0:T(8,128)(2,1)S(1)}, bf16[4,96,384]{2,1,0:T(8,128)(2,1)S(1)}, u32[]{:S(2)}, u32[]{:S(2)}) collective-permute-start(bf16[4,96,384]{2,1,0:T(8,128)(2,1)S(1)} %add_convert_fusion.6.refs_0_), channel_id=1, source_target_pairs={{0,4},{2,6},{4,0},{6,2},{8,12},{10,14},{12,8},{14,10},{16,20},{18,... | collective-permute-start | bytes 884744 | tf_op jit(solution)/shard_map/ppermute | solution.py:23
  353.1 8.6 %collective-permute-start.49 = (bf16[4,96,384]{2,1,0:T(8,128)(2,1)S(1)}, bf16[4,96,384]{2,1,0:T(8,128)(2,1)S(1)}, u32[]{:S(2)}, u32[]{:S(2)}) collective-permute-start(bf16[4,96,384]{2,1,0:T(8,128)(2,1)S(1)} %collective-permute-done.40.refs_1_), channel_id=1, source_target_pairs={{0,4},{2,6},{4,0},{6,2},{8,12},{10,14},{12,8},{14,10},{16,20},{18,... | collective-permute-start | bytes 884744 | tf_op jit(solution)/shard_map/ppermute | solution.py:23
  353.6 10.5 %collective-permute-start.50 = (bf16[4,96,384]{2,1,0:T(8,128)(2,1)S(1)}, bf16[4,96,384]{2,1,0:T(8,128)(2,1)S(1)}, u32[]{:S(2)}, u32[]{:S(2)}) collective-permute-start(bf16[4,96,384]{2,1,0:T(8,128)(2,1)S(1)} %add_convert_fusion.6.refs_0_), channel_id=1, source_target_pairs={{0,2},{2,0},{4,6},{6,4},{8,10},{10,8},{12,14},{14,12},{16,18},{18,... | collective-permute-start | bytes 884744 | tf_op jit(solution)/shard_map/ppermute | solution.py:23
  353.6 10.5 %collective-permute-start.51 = (bf16[4,96,384]{2,1,0:T(8,128)(2,1)S(1)}, bf16[4,96,384]{2,1,0:T(8,128)(2,1)S(1)}, u32[]{:S(2)}, u32[]{:S(2)}) collective-permute-start(bf16[4,96,384]{2,1,0:T(8,128)(2,1)S(1)} %collective-permute-done.40.refs_1_), channel_id=1, source_target_pairs={{0,2},{2,0},{4,6},{6,4},{8,10},{10,8},{12,14},{14,12},{16,18},{18,... | collective-permute-start | bytes 884744 | tf_op jit(solution)/shard_map/ppermute | solution.py:23
  (63 other events, 510.4 us)
where the time goes:
time: 372 us; the launch traced here: 370 us
  Pallas kernels  191 us (51%)
  waiting for transfers between devices  95.8 us (26%)
  starting transfers between devices  40.6 us (11%)
  other arithmetic  28.4 us (8%)
  local copies, waits for them, and re-layouts  13 us (3%)
    ppermute x47, waiting for transfers between devices, swap(): return lax.ppermute(array, 'dp', [(i, i ^ 1 << bit) for i in range(size)])  67.7 us
    pallas_call x1, Pallas kernels, second_half(): pl.pallas_call(second_kernel, grid_spec=pltpu.PrefetchScalarGridSpec(num_...  39 us
    ppermute x47, starting transfers between devices, swap(): return lax.ppermute(array, 'dp', [(i, i ^ 1 << bit) for i in range(size)])  31.2 us
    ppermute x7, waiting for transfers between devices, across(): return lax.ppermute(array, 'tensor', [(0, 1), (1, 0)])  28.2 us
    convert_element_type x16, other arithmetic, add(): return total.astype(LOW)  23.8 us
    pallas_call x2, Pallas kernels, attend_back(): pl.pallas_call(attend_back_kernel, grid=(sequences, pairs), in_specs=[blo...  22.3 us
    pallas_call x2, Pallas kernels, attend(): pl.pallas_call(attend_kernel, grid_spec=pltpu.PrefetchScalarGridSpec(num_...  21.3 us
    pallas_call x1, Pallas kernels, first_half(): pl.pallas_call(first_kernel, grid_spec=pltpu.PrefetchScalarGridSpec(num_s...  20.3 us
  transfers between devices with their start and end apart: 54, of which 16 were waited for; matrix products, arithmetic and copies ran while one was open for 8% of the time, Pallas kernels for 35%

commit v1 on v0

--- a/solution.py
+++ b/solution.py
@@ -30,7 +30,7 @@
 ANYWHERE = pl.BlockSpec(memory_space=pl.ANY)
 
 
-def small_cost(flops=10**6):
+def cost(flops):
     return pl.CostEstimate(flops=flops, bytes_accessed=10**5, transcendentals=0)
 
 
@@ -78,7 +78,7 @@
             jax.ShapeDtypeStruct((rows, width), LOW),
             jax.ShapeDtypeStruct((sequences * pairs * 2, length, length), LOW),
         ],
-        cost_estimate=small_cost(),
+        cost_estimate=cost(10**6),
         name="attend",
     )(bits, lengths, q, k, v)
 
@@ -114,7 +114,7 @@
         + [pl.BlockSpec((2, length, length), lambda s, h: (s * pairs + h, 0, 0))],
         out_specs=pl.BlockSpec((3, length, 128), lambda s, h: (0, s, h)),
         out_shape=jax.ShapeDtypeStruct((3, rows, width), LOW),
-        cost_estimate=small_cost(),
+        cost_estimate=cost(2 * 10**10),
         name="attend_back",
     )(q, k, v, context, grad, probs)
 
@@ -148,7 +148,7 @@
             out_specs=[pl.BlockSpec(attention, place(0, 0, 0)), pl.BlockSpec(forward, place(0, 0))],
         ),
         out_shape=[jax.ShapeDtypeStruct(attention, LOW), jax.ShapeDtypeStruct(forward, LOW)],
-        cost_estimate=small_cost(),
+        cost_estimate=cost(10**6),
         name="pack",
     )(bits, w_qkv, w_out, w_in, w_down)
 
@@ -173,10 +173,11 @@
         self.order, self.size = order, size
         self.here = across(piece)
 
-    def pass_on(self):
-        (self.here,) = self.order.sync(self.here)
+    def pass_on(self, *others):
+        self.here, *others = self.order.sync(self.here, *others)
         self.x = swap(self.here, 1, self.size)
         self.partner = swap(self.here, 0, self.size)
+        return others
 
     def finish(self):
         (self.x,) = self.order.sync(self.x)
@@ -288,7 +289,7 @@
             scratch_shapes=[pltpu.VMEM((3, width, local), LOW), pltpu.SemaphoreType.DMA((4,))],
         ),
         out_shape=[jax.ShapeDtypeStruct((rows, local), LOW)] * 3,
-        cost_estimate=small_cost(),
+        cost_estimate=cost(10**6),
         name="project",
     )(bits, tokens, biases, *parts)
 
@@ -325,7 +326,7 @@
             scratch_shapes=[pltpu.VMEM((3, width, local), LOW)] * 2 + [pltpu.SemaphoreType.DMA((5,))],
         ),
         out_shape=jax.ShapeDtypeStruct((rows, width), LOW),
-        cost_estimate=small_cost(),
+        cost_estimate=cost(2 * 10**10),
         name="project_back",
     )(bits, own, other, grad, weights, *parts)
 
@@ -456,7 +457,7 @@
             jax.ShapeDtypeStruct((rows, hidden), LOW),
             jax.ShapeDtypeStruct((rows, hidden), LOW),
         ],
-        cost_estimate=small_cost(),
+        cost_estimate=cost(10**6),
         name="first_half",
     )(bits, own_context, other_context, tokens, vectors, biases, w_out, w_in, w_down, *parts)
 
@@ -600,7 +601,7 @@
             jax.ShapeDtypeStruct((8, width), WIDE),
             jax.ShapeDtypeStruct((8, hidden), WIDE),
         ],
-        cost_estimate=small_cost(),
+        cost_estimate=cost(10**6),
         name="second_half",
     )(bits, hidden_low, base, cot, slope, normed, scale, vectors, biases, w_out, w_in, w_down, *out_pieces, *pieces)
 
@@ -644,7 +645,7 @@
             ],
         ),
         out_shape=[jax.ShapeDtypeStruct((2,) + piece[1:], LOW)] * 2,
-        cost_estimate=small_cost(),
+        cost_estimate=cost(2 * 10**10),
         name="down_pieces",
     )(bits, activated, grad)
 
@@ -686,7 +687,7 @@
             out_specs=[pl.BlockSpec(piece, lambda i, s: (0, 0, 0, 0))] * 2,
         ),
         out_shape=[jax.ShapeDtypeStruct(piece, LOW)] * 2,
-        cost_estimate=small_cost(),
+        cost_estimate=cost(2 * 10**10),
         name="in_pieces",
     )(bits, hidden_low, grad)
 
@@ -732,7 +733,7 @@
             scratch_shapes=[pltpu.VMEM((8, width // 8, local), WIDE)],
         ),
         out_shape=[jax.ShapeDtypeStruct((4, 4, width // 8, local), LOW)] * 2,
-        cost_estimate=small_cost(),
+        cost_estimate=cost(2 * 10**10),
         name="heads_pieces",
     )(bits, tokens, grads, context, attended)
 
@@ -786,26 +787,33 @@
     def total(self):
         self.kept = self.summed(self.terms["own"])
 
-    def exchange(self, bit):
-        self.terms["own"] = [(array, (), ()) for array in (self.kept, swap(self.kept, bit, self.size))]
+    def exchange(self, bits):
+        if bits:
+            arrived = swap(self.kept, bits[0], self.size)
+            self.terms["own"] = [(array, (), ()) for array in (self.kept, arrived)]
+
+    def fold(self, bits):
+        while bits:
+            bits = bits[1:]
+            self.total()
+            self.exchange(bits)
 
     def spread(self):
-        self.pieces = [self.kept] + [swap(self.kept, bit, self.size) for bit in (2, 1, 0)]
+        self.z, self.x = swap(self.kept, 2, self.size), swap(self.kept, 1, self.size)
 
     def spread_on(self):
-        kept, z, x, partner = self.pieces
-        (z,) = self.order.sync(z)
-        self.pieces = [kept, z, x, swap(z, 1, self.size), partner, swap(z, 0, self.size)]
+        (self.z,) = self.order.sync(self.z)
+        self.far = swap(self.z, 1, self.size)
 
     def finish(self):
-        kept, z, x, xz, partner, partner_z = self.pieces
-        x, xz = self.order.sync(x, xz)
-        return [kept, z, x, xz, partner, partner_z, swap(x, 0, self.size), swap(xz, 0, self.size)]
+        mine = self.order.run(lambda *p: jnp.stack(p), self.kept, self.z, self.x, self.far)
+        return mine, swap(mine, 0, self.size)
 
 
 def widen(bits, pieces, shapes, places):
     def kernel(bits_ref, *refs):
-        sources, outs, (low, wide, semaphores) = refs[:8], refs[8:-3], refs[-3:]
+        outs, (low, wide, semaphores) = refs[2:-3], refs[-3:]
+        sources = [refs[r // 4].at[r % 4] for r in range(8)]
         rank = bits_ref[0] * 4 + bits_ref[1] * 2 + bits_ref[2]
         loads = [pltpu.make_async_copy(sources[r], low.at[r], semaphores.at[r]) for r in range(8)]
         for load in loads:
@@ -821,13 +829,13 @@
         for store in stores:
             store.wait()
 
-    piece = pieces[0].shape
+    piece = pieces[0].shape[1:]
     return pl.pallas_call(
         kernel,
         grid_spec=pltpu.PrefetchScalarGridSpec(
             num_scalar_prefetch=1,
             grid=(1,),
-            in_specs=[ANYWHERE] * 8,
+            in_specs=[ANYWHERE] * 2,
             out_specs=[ANYWHERE] * len(shapes),
             scratch_shapes=[
                 pltpu.VMEM((8,) + piece, LOW),
@@ -836,7 +844,7 @@
             ],
         ),
         out_shape=[jax.ShapeDtypeStruct(shape, WIDE) for shape in shapes],
-        cost_estimate=small_cost(),
+        cost_estimate=cost(2 * 10**10),
         name="widen",
     )(bits, *pieces)
 
@@ -891,10 +899,10 @@
     qkv_own = jnp.transpose(w_qkv, (1, 0, 2))
     attention_piece, forward_piece = pack(bits, qkv_own, w_out, w_in, w_down)
     order = Order(attention_piece)
-    attention_fetch = Fetch(order, attention_piece, size)
     biases = order.run(
         lambda *vectors: jnp.concatenate([v.reshape(-1, local) for v in vectors]), q_bias, v_bias, in_bias
     )
+    attention_fetch = Fetch(order, attention_piece, size)
     vectors = order.run(
         lambda *vectors: jnp.stack(vectors), out_bias, gain_one, shift_one, down_bias, gain_two, shift_two
     )
@@ -903,7 +911,7 @@
     forward_fetch = Fetch(order, forward_piece, size)
 
     q_own, k_own, v_own = order.run(lambda x: project(bits, x, biases, [qkv_own]), tokens)
-    attention_fetch.pass_on()
+    (biases_other,) = attention_fetch.pass_on(biases_other)
     context_own, probs_own = order.run(
         lambda *qkv: attend(bits, lengths, *qkv), q_own, k_own, v_own
     )
@@ -1000,13 +1008,12 @@
     entry.halve("own", "z")
     down.halve("own", "z")
     heads.begin("own", *heads_grad(project_own, context_own))
+    entry.total()
+    entry.exchange(extra)
+    down.total()
+    down.exchange(extra)
+    heads.halve("own", "x")
     arrived = across(other_sums)
-    entry.total()
-    if extra:
-        entry.exchange(extra[0])
-    down.total()
-    if extra:
-        down.exchange(extra[0])
     input_grad = order.run(
         lambda *grads: project_back(bits, *grads, attended_grad, qkv_own, attention_pieces),
         project_own,
@@ -1021,42 +1028,34 @@
         sums,
         arrived,
     )
+    heads.halve("own", "z")
+    entry.fold(extra)
+    entry.spread()
     arrived = swap(totals, 0, size)
-    heads.halve("own", "x")
+    heads.total()
+    heads.exchange(extra)
+    down.fold(extra)
+    down.spread()
+    entry.spread_on()
     totals = order.run(jnp.add, totals, arrived)
+    down.spread_on()
     arrived = swap(totals, 1, size)
+    entry_pieces = entry.finish()
+    (grad_w_in,) = order.run(
+        lambda *pieces: widen(bits, pieces, [(width, hidden)], in_places), *entry_pieces
+    )
+    heads.fold(extra)
+    totals = order.run(jnp.add, totals, arrived)
+    heads.spread()
+    arrived = swap(totals, 2, size)
+    (grad_w_down,) = order.run(
+        lambda *pieces: widen(bits, pieces, [(hidden, width)], down_places), *down.finish()
+    )
+    totals = order.run(jnp.add, totals, arrived)
+    heads.spread_on()
     for bit in extra:
-        entry.total()
-        if bit + 1 in extra:
-            entry.exchange(bit + 1)
-        down.total()
-        if bit + 1 in extra:
-            down.exchange(bit + 1)
-    entry.spread()
-    down.spread()
-    totals = order.run(jnp.add, totals, arrived)
-    arrived = swap(totals, 2, size)
-    heads.halve("own", "z")
-    entry.spread_on()
-    down.spread_on()
-    totals = order.run(jnp.add, totals, arrived)
-    heads.total()
-    entry_pieces = entry.finish()
-    down_pieces_all = down.finish()
-    for bit in extra:
-        heads.exchange(bit)
         arrived = swap(totals, bit, size)
-        if bit == extra[0]:
-            (grad_w_in,) = order.run(
-                lambda *pieces: widen(bits, pieces, [(width, hidden)], in_places), *entry_pieces
-            )
         totals = order.run(jnp.add, totals, arrived)
-        heads.total()
-    heads.spread()
-    (grad_w_down,) = order.run(
-        lambda *pieces: widen(bits, pieces, [(hidden, width)], down_places), *down_pieces_all
-    )
-    heads.spread_on()
     count = 6 * width
     shared = totals[:count].reshape(6, width)
     grad_in_bias = totals[count : count + hidden]

time: 372 us -> 345 us (0.927)
  waiting for transfers between devices: 95.8 us -> 81.1 us
  other arithmetic: 28.4 us -> 23.7 us
  local copies, waits for them, and re-layouts: 13 us -> 8.49 us
    ppermute x7, waiting for transfers between devices: 28.2 us -> 9.91 us  [across(): return lax.ppermute(array, 'tensor', [(0, 1), (1, 0)])]
    convert_element_type x16, other arithmetic: 23.8 us -> 17.9 us  [add(): return total.astype(LOW)]
    ppermute x47 -> x38, waiting for transfers between devices: 67.7 us -> 71.2 us  [swap(): return lax.ppermute(array, 'dp', [(i, i ^ 1 << bit) for i in range(size)])]
    unnamed x114 -> x70, local copies, waits for them, and re-layouts: 8.28 us -> 4.99 us
    ppermute x47 -> x38, starting transfers between devices: 31.2 us -> 28.5 us  [swap(): return lax.ppermute(array, 'dp', [(i, i ^ 1 << bit) for i in range(size)])]
  transfers between devices with their start and end apart: 54 -> 45, of which waited for: 16 -> 19; matrix products, arithmetic and copies ran while one was open for 8% -> 7% of each run, Pallas kernels for 35% -> 37%
where the time goes in v1:
time: 345 us; the launch traced here: 343 us
  Pallas kernels  190 us (55%)
  waiting for transfers between devices  81.1 us (24%)
  starting transfers between devices  38.2 us (11%)
  other arithmetic  23.7 us (7%)
  local copies, waits for them, and re-layouts  8.49 us (2%)
    ppermute x38, waiting for transfers between devices, swap(): return lax.ppermute(array, 'dp', [(i, i ^ 1 << bit) for i in range(size)])  71.2 us
    pallas_call x1, Pallas kernels, second_half(): pl.pallas_call(second_kernel, grid_spec=pltpu.PrefetchScalarGridSpec(num_...  38.9 us
    ppermute x38, starting transfers between devices, swap(): return lax.ppermute(array, 'dp', [(i, i ^ 1 << bit) for i in range(size)])  28.5 us
    pallas_call x2, Pallas kernels, attend_back(): pl.pallas_call(attend_back_kernel, grid=(sequences, pairs), in_specs=[blo...  22.4 us
    pallas_call x2, Pallas kernels, attend(): pl.pallas_call(attend_kernel, grid_spec=pltpu.PrefetchScalarGridSpec(num_...  21.1 us
    pallas_call x1, Pallas kernels, first_half(): pl.pallas_call(first_kernel, grid_spec=pltpu.PrefetchScalarGridSpec(num_s...  20.3 us
    convert_element_type x16, other arithmetic, add(): return total.astype(LOW)  17.9 us
    pallas_call x2, Pallas kernels, heads_pieces(): pl.pallas_call(heads_kernel, grid_spec=pltpu.PrefetchScalarGridSpec(num_s...  16.8 us
  transfers between devices with their start and end apart: 45, of which 19 were waited for; matrix products, arithmetic and copies ran while one was open for 7% of the time, Pallas kernels for 37%

profile of v1, /device:TPU:0, one launch (start us, length us, event | category | flops | bytes accessed | tf_op | source)
XLA Modules:
  0.0 343.4 jit_solution(11487238809298299720)
XLA Ops:
  1.3 3.5 %pack.1 = (bf16[4,192,384]{2,1,0:T(8,128)(2,1)}, bf16[768,768]{1,0:T(8,128)(2,1)}) custom-call(s32[4]{0:T(128)} %pad_add_fusion.bits_ref, bf16[3,768,384]{2,1,0:T(8,128)(2,1)} %bitcast.72, bf16[384,768]{1,0:T(8,128)(2,1)} %w_out_ref.3, bf16[768,1536]{1,0:T(8,128)(2,1)} %w_in_ref.3, bf16[1536,768]{1,0:T(8,128)(2,1)} %w_down_ref.3), custom_call_target="tpu_custom_call" | custom-call | flops 1000000 | bytes 100000 | tf_op jit(solution)/shard_map/pack/pallas_call | solution.py:141
  4.8 3.0 collective-permute-start
  8.4 7.1 %project.2 = (bf16[1024,384]{1,0:T(8,128)(2,1)}, bf16[1024,384]{1,0:T(8,128)(2,1)}, bf16[1024,384]{1,0:T(8,128)(2,1)}) custom-call(s32[4]{0:T(128)} %pad_add_fusion.bits_ref, bf16[2048,768]{1,0:T(8,128)(2,1)} %x_ref.8, f32[6,384]{1,0:T(8,128)} %copy-done.21, bf16[3,768,384]{2,1,0:T(8,128)(2,1)} %bitcast.73), custom_call_target="tpu_custom_call" | custom-call | flops 1000000 | bytes 100000 | tf_op jit(solution)/shard_map/project/pallas_call | solution.py:278
  15.5 6.0 %collective-permute-done.1.biases_ref = f32[6,384]{1,0:T(8,128)S(1)} collective-permute-done((f32[6,384]{1,0:T(8,128)S(1)}, f32[6,384]{1,0:T(8,128)S(1)}, u32[]{:S(2)}, u32[]{:S(2)}) %collective-permute-start.1) | collective-permute-done | bytes 9248 | tf_op jit(solution)/shard_map/ppermute | solution.py:27
  22.1 1.7 collective-permute-start.2
  26.1 10.6 %attend.2 = (bf16[1024,384]{1,0:T(8,128)(2,1)}, bf16[12,512,512]{2,1,0:T(8,128)(2,1)}) custom-call(s32[4]{0:T(128)} %pad_add_fusion.bits_ref, s32[4]{0:T(128)} %length_ref.3, bf16[1024,384]{1,0:T(8,128)(2,1)} %get-tuple-element.292.q_ref, bf16[1024,384]{1,0:T(8,128)(2,1)} %get-tuple-element.293.k_ref, bf16[1024,384]{1,0:T(8,128)(2,1)} %get-tuple-element.200.v_ref), custom_call_target="tpu_custom_call" | custom-call | flops 1000000 | bytes 100000 | tf_op jit(solution)/shard_map/attend/pallas_call | solution.py:66
  40.3 7.1 %project.3 = (bf16[1024,384]{1,0:T(8,128)(2,1)}, bf16[1024,384]{1,0:T(8,128)(2,1)}, bf16[1024,384]{1,0:T(8,128)(2,1)}) custom-call(s32[4]{0:T(128)} %pad_add_fusion.bits_ref, bf16[2048,768]{1,0:T(8,128)(2,1)} %x_ref.8, f32[6,384]{1,0:T(8,128)} %copy-done.24, bf16[4,192,384]{2,1,0:T(8,128)(2,1)} %copy-done, bf16[4,192,384]{2,1,0:T(8,128)(2,1)} %copy-done.1, ...), custom_call_target="tpu_custom_call" | custom-call | flops 1000000 | bytes 100000 | tf_op jit(solution)/shard_map/project/pallas_call | solution.py:278
  47.5 3.9 %collective-permute-done.5.refs_4_ = bf16[768,768]{1,0:T(8,128)(2,1)S(1)} collective-permute-done((bf16[768,768]{1,0:T(8,128)(2,1)}, bf16[768,768]{1,0:T(8,128)(2,1)S(1)}, u32[]{:S(2)}, u32[]{:S(2)}) %collective-permute-start.5) | collective-permute-done | bytes 1179680 | tf_op jit(solution)/shard_map/ppermute | solution.py:27
  52.0 10.6 %attend.3 = (bf16[1024,384]{1,0:T(8,128)(2,1)}, bf16[12,512,512]{2,1,0:T(8,128)(2,1)}) custom-call(s32[4]{0:T(128)} %pad_add_fusion.bits_ref, s32[4]{0:T(128)} %length_ref.3, bf16[1024,384]{1,0:T(8,128)(2,1)} %get-tuple-element.266.q_ref, bf16[1024,384]{1,0:T(8,128)(2,1)} %get-tuple-element.267.k_ref, bf16[1024,384]{1,0:T(8,128)(2,1)} %get-tuple-element.213.v_ref), custom_call_target="tpu_custom_call" | custom-call | flops 1000000 | bytes 100000 | tf_op jit(solution)/shard_map/attend/pallas_call | solution.py:66
  62.6 20.3 %first_half.1 = (bf16[1024,768]{1,0:T(8,128)(2,1)}, bf16[1024,768]{1,0:T(8,128)(2,1)}, f32[1024,1]{1,0:T(8,128)}, f32[1024,768]{1,0:T(8,128)}, bf16[1024,1536]{1,0:T(8,128)(2,1)}, /*index=5*/bf16[1024,1536]{1,0:T(8,128)(2,1)}) custom-call(s32[4]{0:T(128)} %pad_add_fusion.bits_ref, bf16[1024,384]{1,0:T(8,128)(2,1)} %get-tuple-element.295.own_context_ref.context_ref, ...), custom_call_target="tpu_custom_call" | custom-call | flops 1000000 | bytes 100000 | tf_op jit(solution)/shard_map/first_half/pallas_call | solution.py:427
  83.4 2.5 collective-permute-done.8.refs_7_
  86.9 38.9 %second_half.1 = (bf16[1024,768]{1,0:T(8,128)(2,1)}, bf16[1024,768]{1,0:T(8,128)(2,1)}, bf16[1024,1536]{1,0:T(8,128)(2,1)}, bf16[1024,1536]{1,0:T(8,128)(2,1)}, ...) custom-call(s32[4]{0:T(128)} %pad_add_fusion.bits_ref, ...), custom_call_target="tpu_custom_call" | custom-call | flops 1000000 | bytes 100000 | tf_op jit(solution)/shard_map/second_half/pallas_call | solution.py:555
  125.9 7.5 %down_pieces.2 = (bf16[2,2,192,768]{3,2,1,0:T(8,128)(2,1)}, bf16[2,2,192,768]{3,2,1,0:T(8,128)(2,1)}) custom-call(s32[4]{0:T(128)} %pad_add_fusion.bits_ref, bf16[1024,1536]{1,0:T(8,128)(2,1)} %get-tuple-element.250.act_ref, bf16[1024,768]{1,0:T(8,128)(2,1)} %get-tuple-element.251.grad_ref), custom_call_target="tpu_custom_call" | custom-call | flops 20000000000 | bytes 100000 | tf_op jit(solution)/shard_map/down_pieces/pallas_call | solution.py:631
  133.7 7.2 %in_pieces.2 = (bf16[2,2,384,384]{3,2,1,0:T(8,128)(2,1)}, bf16[2,2,384,384]{3,2,1,0:T(8,128)(2,1)}) custom-call(s32[4]{0:T(128)} %pad_add_fusion.bits_ref, bf16[1024,768]{1,0:T(8,128)(2,1)} %get-tuple-element.229.hidden_ref, bf16[1024,1536]{1,0:T(8,128)(2,1)} %get-tuple-element.253.grad_ref), custom_call_target="tpu_custom_call" | custom-call | flops 20000000000 | bytes 100000 | tf_op jit(solution)/shard_map/in_pieces/pallas_call | solution.py:678
  142.9 7.3 %in_pieces.3 = (bf16[2,2,384,384]{3,2,1,0:T(8,128)(2,1)}, bf16[2,2,384,384]{3,2,1,0:T(8,128)(2,1)}) custom-call(s32[4]{0:T(128)} %pad_add_fusion.bits_ref, bf16[1024,768]{1,0:T(8,128)(2,1)} %get-tuple-element.229.hidden_ref, bf16[1024,1536]{1,0:T(8,128)(2,1)} %get-tuple-element.260.grad_ref), custom_call_target="tpu_custom_call" | custom-call | flops 20000000000 | bytes 100000 | tf_op jit(solution)/shard_map/in_pieces/pallas_call | solution.py:678
  150.2 2.0 fusion.1
  153.8 7.4 %down_pieces.3 = (bf16[2,2,192,768]{3,2,1,0:T(8,128)(2,1)}, bf16[2,2,192,768]{3,2,1,0:T(8,128)(2,1)}) custom-call(s32[4]{0:T(128)} %pad_add_fusion.bits_ref, bf16[1024,1536]{1,0:T(8,128)(2,1)} %get-tuple-element.264.act_ref, bf16[1024,768]{1,0:T(8,128)(2,1)} %get-tuple-element.251.grad_ref), custom_call_target="tpu_custom_call" | custom-call | flops 20000000000 | bytes 100000 | tf_op jit(solution)/shard_map/down_pieces/pallas_call | solution.py:631
  161.4 11.3 %attend_back.2.grads_ref.other_ref = bf16[3,1024,384]{2,1,0:T(8,128)(2,1)} custom-call(bf16[1024,384]{1,0:T(8,128)(2,1)} %get-tuple-element.266.q_ref, bf16[1024,384]{1,0:T(8,128)(2,1)} %get-tuple-element.267.k_ref, bf16[1024,384]{1,0:T(8,128)(2,1)} %get-tuple-element.213.v_ref, bf16[1024,384]{1,0:T(8,128)(2,1)} %get-tuple-element.269.other_context_ref.context_ref, ...), custom_call_target="tpu_custom_call" | custom-call | flops 20000000000 | bytes 100000 | tf_op jit(solution)/shard_map/attend_back/pallas_call | solution.py:110
  174.6 2.3 fusion
  176.9 2.3 fusion.3
  179.2 8.4 %heads_pieces.2 = (bf16[4,4,96,384]{3,2,1,0:T(8,128)(2,1)}, bf16[4,4,96,384]{3,2,1,0:T(8,128)(2,1)}) custom-call(s32[4]{0:T(128)} %pad_add_fusion.bits_ref, bf16[2048,768]{1,0:T(8,128)(2,1)} %x_ref.8, bf16[3,1024,384]{2,1,0:T(8,128)(2,1)} %attend_back.2.grads_ref.other_ref, bf16[1024,384]{1,0:T(8,128)(2,1)} %get-tuple-element.269.other_context_ref.context_ref, ...), custom_call_target="tpu_custom_call" | custom-call | flops 20000000000 | bytes 100000 | tf_op jit(solution)/shard_map/heads_pieces/pallas_call | solution.py:721
  191.5 1.6 convert_reduce_fusion.3
  194.0 1.6 collective-permute-start.16
  195.6 11.1 %attend_back.3.grads_ref.own_ref = bf16[3,1024,384]{2,1,0:T(8,128)(2,1)} custom-call(bf16[1024,384]{1,0:T(8,128)(2,1)} %get-tuple-element.292.q_ref, bf16[1024,384]{1,0:T(8,128)(2,1)} %get-tuple-element.293.k_ref, bf16[1024,384]{1,0:T(8,128)(2,1)} %get-tuple-element.200.v_ref, bf16[1024,384]{1,0:T(8,128)(2,1)} %get-tuple-element.295.own_context_ref.context_ref, ...), custom_call_target="tpu_custom_call" | custom-call | flops 20000000000 | bytes 100000 | tf_op jit(solution)/shard_map/attend_back/pallas_call | solution.py:110
  208.1 9.5 %collective-permute-done.17 = bf16[2,192,768]{2,1,0:T(8,128)(2,1)} collective-permute-done((bf16[2,192,768]{2,1,0:T(8,128)(2,1)}, bf16[2,192,768]{2,1,0:T(8,128)(2,1)}, u32[]{:S(2)}, u32[]{:S(2)}) %collective-permute-start.17) | collective-permute-done | bytes 589856 | tf_op jit(solution)/shard_map/ppermute | solution.py:23
  219.0 8.3 %heads_pieces.3 = (bf16[4,4,96,384]{3,2,1,0:T(8,128)(2,1)}, bf16[4,4,96,384]{3,2,1,0:T(8,128)(2,1)}) custom-call(s32[4]{0:T(128)} %pad_add_fusion.bits_ref, bf16[2048,768]{1,0:T(8,128)(2,1)} %x_ref.8, bf16[3,1024,384]{2,1,0:T(8,128)(2,1)} %attend_back.3.grads_ref.own_ref, bf16[1024,384]{1,0:T(8,128)(2,1)} %get-tuple-element.295.own_context_ref.context_ref, ...), custom_call_target="tpu_custom_call" | custom-call | flops 20000000000 | bytes 100000 | tf_op jit(solution)/shard_map/heads_pieces/pallas_call | solution.py:721
  227.3 1.6 collective-permute-start.22
  230.8 6.3 %collective-permute-done.22 = bf16[384,384]{1,0:T(8,128)(2,1)S(1)} collective-permute-done((bf16[384,384]{1,0:T(8,128)(2,1)S(1)}, bf16[384,384]{1,0:T(8,128)(2,1)S(1)}, u32[]{:S(2)}, u32[]{:S(2)}) %collective-permute-start.22) | collective-permute-done | bytes 294944 | tf_op jit(solution)/shard_map/ppermute | solution.py:23
  238.4 2.7 collective-permute-start.26
  241.1 5.7 %collective-permute-done.21 = bf16[192,768]{1,0:T(8,128)(2,1)S(1)} collective-permute-done((bf16[192,768]{1,0:T(8,128)(2,1)S(1)}, bf16[192,768]{1,0:T(8,128)(2,1)S(1)}, u32[]{:S(2)}, u32[]{:S(2)}) %collective-permute-start.21) | collective-permute-done | bytes 294944 | tf_op jit(solution)/shard_map/ppermute | solution.py:23
  248.3 1.7 fusion.4
  250.6 11.7 %project_back.1 = bf16[1024,768]{1,0:T(8,128)(2,1)} custom-call(s32[4]{0:T(128)} %pad_add_fusion.bits_ref, bf16[3,1024,384]{2,1,0:T(8,128)(2,1)} %attend_back.3.grads_ref.own_ref, bf16[3,1024,384]{2,1,0:T(8,128)(2,1)} %attend_back.2.grads_ref.other_ref, bf16[1024,768]{1,0:T(8,128)(2,1)} %get-tuple-element.283.attended_ref.grad_ref, ...), custom_call_target="tpu_custom_call" | custom-call | flops 20000000000 | bytes 100000 | tf_op jit(solution)/shard_map/project_back/pallas_call | solution.py:319
  262.4 1.6 convert_reduce_fusion.1
  266.3 1.9 collective-permute-start.29
  269.7 12.1 %collective-permute-done.25 = bf16[4,96,384]{2,1,0:T(8,128)(2,1)S(1)} collective-permute-done((bf16[4,96,384]{2,1,0:T(8,128)(2,1)S(1)}, bf16[4,96,384]{2,1,0:T(8,128)(2,1)S(1)}, u32[]{:S(2)}, u32[]{:S(2)}) %collective-permute-start.25) | collective-permute-done | bytes 294944 | tf_op jit(solution)/shard_map/ppermute | solution.py:23
  283.2 3.8 %collective-permute-done.28 = bf16[384,384]{1,0:T(8,128)(2,1)S(1)} collective-permute-done((bf16[384,384]{1,0:T(8,128)(2,1)S(1)}, bf16[384,384]{1,0:T(8,128)(2,1)S(1)}, u32[]{:S(2)}, u32[]{:S(2)}) %collective-permute-start.28) | collective-permute-done | bytes 294944 | tf_op jit(solution)/shard_map/ppermute | solution.py:23
  288.5 6.4 %collective-permute-done.31 = bf16[384,384]{1,0:T(8,128)(2,1)S(1)} collective-permute-done((bf16[384,384]{1,0:T(8,128)(2,1)S(1)}, bf16[384,384]{1,0:T(8,128)(2,1)S(1)}, u32[]{:S(2)}, u32[]{:S(2)}) %collective-permute-start.31) | collective-permute-done | bytes 294944 | tf_op jit(solution)/shard_map/ppermute | solution.py:23
  295.7 2.3 collective-permute-done.34
  300.4 5.4 %collective-permute-done.37 = bf16[192,768]{1,0:T(8,128)(2,1)S(1)} collective-permute-done((bf16[192,768]{1,0:T(8,128)(2,1)S(1)}, bf16[192,768]{1,0:T(8,128)(2,1)S(1)}, u32[]{:S(2)}, u32[]{:S(2)}) %collective-permute-start.37) | collective-permute-done | bytes 294944 | tf_op jit(solution)/shard_map/ppermute | solution.py:23
  307.2 4.0 %widen.3 = f32[768,1536]{1,0:T(8,128)} custom-call(s32[4]{0:T(128)} %pad_add_fusion.bits_ref, bf16[4,384,384]{2,1,0:T(8,128)(2,1)} %copy-done.15, bf16[4,384,384]{2,1,0:T(8,128)(2,1)} %collective-permute-done.32.refs_1_), custom_call_target="tpu_custom_call" | custom-call | flops 20000000000 | bytes 100000 | tf_op jit(solution)/shard_map/widen/pallas_call | solution.py:833
  311.2 4.6 %collective-permute-done.27 = bf16[4,96,384]{2,1,0:T(8,128)(2,1)S(1)} collective-permute-done((bf16[4,96,384]{2,1,0:T(8,128)(2,1)S(1)}, bf16[4,96,384]{2,1,0:T(8,128)(2,1)S(1)}, u32[]{:S(2)}, u32[]{:S(2)}) %collective-permute-start.27) | collective-permute-done | bytes 294944 | tf_op jit(solution)/shard_map/ppermute | solution.py:23
  316.2 1.6 collective-permute-start.41
  317.8 1.9 collective-permute-start.33
  319.8 4.0 %widen.4 = f32[1536,768]{1,0:T(8,128)} custom-call(s32[4]{0:T(128)} %pad_add_fusion.bits_ref, bf16[4,192,768]{2,1,0:T(8,128)(2,1)} %copy-done.17, bf16[4,192,768]{2,1,0:T(8,128)(2,1)} %collective-permute-done.40.refs_1_), custom_call_target="tpu_custom_call" | custom-call | flops 20000000000 | bytes 100000 | tf_op jit(solution)/shard_map/widen/pallas_call | solution.py:833
  323.8 3.0 collective-permute-done.33
  328.9 3.5 %collective-permute-done.43 = f32[6912]{0:T(1024)S(1)} collective-permute-done((f32[6912]{0:T(1024)S(1)}, f32[6912]{0:T(1024)S(1)}, u32[]{:S(2)}, u32[]{:S(2)}) %collective-permute-start.43) | collective-permute-done | bytes 27680 | tf_op jit(solution)/shard_map/ppermute | solution.py:23
  332.5 2.5 collective-permute-done.42
  339.1 4.0 %widen.5 = (f32[3,768,384]{2,1,0:T(8,128)}, f32[384,768]{1,0:T(8,128)}) custom-call(s32[4]{0:T(128)} %pad_add_fusion.bits_ref, bf16[4,4,96,384]{3,2,1,0:T(8,128)(2,1)} %copy-done.16, bf16[4,4,96,384]{3,2,1,0:T(8,128)(2,1)} %copy-done.34), custom_call_target="tpu_custom_call" | custom-call | flops 20000000000 | bytes 100000 | tf_op jit(solution)/shard_map/widen/pallas_call | solution.py:833
  (176 shorter events, 46.4 us)
Async XLA Ops:
  4.8 16.8 %collective-permute-start = (bf16[4,192,384]{2,1,0:T(8,128)(2,1)}, bf16[4,192,384]{2,1,0:T(8,128)(2,1)S(1)}, u32[]{:S(2)}, u32[]{:S(2)}) collective-permute-start(bf16[4,192,384]{2,1,0:T(8,128)(2,1)} %get-tuple-element.194), channel_id=1, source_target_pairs={{0,1},{1,0},{2,3},{3,2},{4,5},{5,4},{6,7},{7,6},{8,9},{9,8},{10,11... | collective-permute-start | bytes 1769480 | tf_op jit(solution)/shard_map/ppermute | solution.py:27
  7.8 13.7 %collective-permute-start.1 = (f32[6,384]{1,0:T(8,128)S(1)}, f32[6,384]{1,0:T(8,128)S(1)}, u32[]{:S(2)}, u32[]{:S(2)}) collective-permute-start(f32[6,384]{1,0:T(8,128)S(1)} %pad_maximum_fusion.4.biases_ref), channel_id=1, source_target_pairs={{0,1},{1,0},{2,3},{3,2},{4,5},{5,4},{6,7},{7,6},{8,9},{9,8},{10,11... | collective-permute-start | bytes 27656 | tf_op jit(solution)/shard_map/ppermute | solution.py:27
  8.4 15.5 %copy-start.29 = (f32[768]{0:T(1024)S(1)}, f32[768]{0:T(1024)}, u32[]{:S(2)}) copy-start(f32[768]{0:T(1024)} %param.28) | copy-start | bytes 9220
  8.4 15.5 %copy-start.30 = (f32[768]{0:T(1024)S(1)}, f32[768]{0:T(1024)}, u32[]{:S(2)}) copy-start(f32[768]{0:T(1024)} %param.29) | copy-start | bytes 9220
  8.4 15.5 %copy-start.31 = (f32[768]{0:T(1024)S(1)}, f32[768]{0:T(1024)}, u32[]{:S(2)}) copy-start(f32[768]{0:T(1024)} %param.30) | copy-start | bytes 9220
  22.1 14.5 %collective-permute-start.2 = (bf16[4,192,384]{2,1,0:T(8,128)(2,1)S(1)}, bf16[4,192,384]{2,1,0:T(8,128)(2,1)S(1)}, u32[]{:S(2)}, u32[]{:S(2)}) collective-permute-start(bf16[4,192,384]{2,1,0:T(8,128)(2,1)S(1)} %collective-permute-done.refs_0_), channel_id=1, source_target_pairs={{0,4},{2,6},{4,0},{6,2},{8,12},{10,14},{12,8},{14,10},{16,20},{18,... | collective-permute-start | bytes 1769480 | tf_op jit(solution)/shard_map/ppermute | solution.py:23
  24.6 26.8 %collective-permute-start.5 = (bf16[768,768]{1,0:T(8,128)(2,1)}, bf16[768,768]{1,0:T(8,128)(2,1)S(1)}, u32[]{:S(2)}, u32[]{:S(2)}) collective-permute-start(bf16[768,768]{1,0:T(8,128)(2,1)} %get-tuple-element.225), channel_id=1, source_target_pairs={{0,1},{1,0},{2,3},{3,2},{4,5},{5,4},{6,7},{7,6},{8,9},{9,8},{10,11... | collective-permute-start | bytes 3538952 | tf_op jit(solution)/shard_map/ppermute | solution.py:27
  36.7 2.0 collective-permute-start.3
  36.7 2.8 collective-permute-start.4
  51.4 31.5 %collective-permute-start.6 = (bf16[768,768]{1,0:T(8,128)(2,1)S(1)}, bf16[768,768]{1,0:T(8,128)(2,1)S(1)}, u32[]{:S(2)}, u32[]{:S(2)}) collective-permute-start(bf16[768,768]{1,0:T(8,128)(2,1)S(1)} %collective-permute-done.5.refs_4_), channel_id=1, source_target_pairs={{0,4},{2,6},{4,0},{6,2},{8,12},{10,14},{12,8},{14,10},{16,20},{18,... | collective-permute-start | bytes 3538952 | tf_op jit(solution)/shard_map/ppermute | solution.py:23
  52.0 31.4 %collective-permute-start.7 = (bf16[768,768]{1,0:T(8,128)(2,1)S(1)}, bf16[768,768]{1,0:T(8,128)(2,1)S(1)}, u32[]{:S(2)}, u32[]{:S(2)}) collective-permute-start(bf16[768,768]{1,0:T(8,128)(2,1)S(1)} %collective-permute-done.5.refs_4_), channel_id=1, source_target_pairs={{0,2},{2,0},{4,6},{6,4},{8,10},{10,8},{12,14},{14,12},{16,18},{18,... | collective-permute-start | bytes 3538952 | tf_op jit(solution)/shard_map/ppermute | solution.py:23
  82.9 3.0 collective-permute-start.8
  133.3 7.8 %collective-permute-start.10 = (bf16[2,2,192,768]{3,2,1,0:T(8,128)(2,1)}, bf16[2,2,192,768]{3,2,1,0:T(8,128)(2,1)S(1)}, u32[]{:S(2)}, u32[]{:S(2)}) collective-permute-start(bf16[2,2,192,768]{3,2,1,0:T(8,128)(2,1)} %get-tuple-element.252), channel_id=1, source_target_pairs={{0,2},{2,0},{4,6},{6,4},{8,10},{10,8},{12,14},{14,12},{16,18},{18,... | collective-permute-start | bytes 3538952 | tf_op jit(solution)/shard_map/ppermute | solution.py:23
  141.0 9.3 %collective-permute-start.9 = (bf16[2,2,384,384]{3,2,1,0:T(8,128)(2,1)}, bf16[2,2,384,384]{3,2,1,0:T(8,128)(2,1)}, u32[]{:S(2)}, u32[]{:S(2)}) collective-permute-start(bf16[2,2,384,384]{3,2,1,0:T(8,128)(2,1)} %get-tuple-element.255), channel_id=1, source_target_pairs={{0,2},{2,0},{4,6},{6,4},{8,10},{10,8},{12,14},{14,12},{16,18},{18,... | collective-permute-start | bytes 3538952 | tf_op jit(solution)/shard_map/ppermute | solution.py:23
  141.4 35.5 %collective-permute-start.11 = (bf16[2,2,192,768]{3,2,1,0:T(8,128)(2,1)S(1)}, bf16[2,2,192,768]{3,2,1,0:T(8,128)(2,1)}, u32[]{:S(2)}, u32[]{:S(2)}) collective-permute-start(bf16[2,2,192,768]{3,2,1,0:T(8,128)(2,1)S(1)} %add_convert_fusion.1), channel_id=1, source_target_pairs={{0,1},{1,0},{2,3},{3,2},{4,5},{5,4},{6,7},{7,6},{8,9},{9,8},{10,11... | collective-permute-start | bytes 3538952 | tf_op jit(solution)/shard_map/ppermute | solution.py:27
  150.2 22.5 %collective-permute-start.14 = (bf16[2,2,384,384]{3,2,1,0:T(8,128)(2,1)}, bf16[2,2,384,384]{3,2,1,0:T(8,128)(2,1)S(1)}, u32[]{:S(2)}, u32[]{:S(2)}) collective-permute-start(bf16[2,2,384,384]{3,2,1,0:T(8,128)(2,1)} %get-tuple-element.261), channel_id=1, source_target_pairs={{0,2},{2,0},{4,6},{6,4},{8,10},{10,8},{12,14},{14,12},{16,18},{18,... | collective-permute-start | bytes 3538952 | tf_op jit(solution)/shard_map/ppermute | solution.py:23
  152.3 21.4 %collective-permute-start.13 = (bf16[2,384,384]{2,1,0:T(8,128)(2,1)}, bf16[2,384,384]{2,1,0:T(8,128)(2,1)}, u32[]{:S(2)}, u32[]{:S(2)}) collective-permute-start(bf16[2,384,384]{2,1,0:T(8,128)(2,1)} %fusion.1), channel_id=1, source_target_pairs={{0,4},{2,6},{4,0},{6,2},{8,12},{10,14},{12,8},{14,10},{16,20},{18,... | collective-permute-start | bytes 1769480 | tf_op jit(solution)/shard_map/ppermute | solution.py:23
  161.2 15.7 %collective-permute-start.12 = (bf16[2,2,192,768]{3,2,1,0:T(8,128)(2,1)}, bf16[2,2,192,768]{3,2,1,0:T(8,128)(2,1)}, u32[]{:S(2)}, u32[]{:S(2)}) collective-permute-start(bf16[2,2,192,768]{3,2,1,0:T(8,128)(2,1)} %get-tuple-element.265), channel_id=1, source_target_pairs={{0,2},{2,0},{4,6},{6,4},{8,10},{10,8},{12,14},{14,12},{16,18},{18,... | collective-permute-start | bytes 3538952 | tf_op jit(solution)/shard_map/ppermute | solution.py:23
  187.6 6.1 %collective-permute-start.15 = (bf16[2,2,4,96,384]{4,3,2,1,0:T(8,128)(2,1)}, bf16[2,2,4,96,384]{4,3,2,1,0:T(8,128)(2,1)S(1)}, u32[]{:S(2)}, u32[]{:S(2)}) collective-permute-start(bf16[2,2,4,96,384]{4,3,2,1,0:T(8,128)(2,1)} %bitcast.94), channel_id=1, source_target_pairs={{0,2},{2,0},{4,6},{6,4},{8,10},{10,8},{12,14},{14,12},{16,18},{18,... | collective-permute-start | bytes 3538952 | tf_op jit(solution)/shard_map/ppermute | solution.py:23
  188.9 17.9 %collective-permute-start.19 = (bf16[2,384,384]{2,1,0:T(8,128)(2,1)}, bf16[2,384,384]{2,1,0:T(8,128)(2,1)}, u32[]{:S(2)}, u32[]{:S(2)}) collective-permute-start(bf16[2,384,384]{2,1,0:T(8,128)(2,1)} %fusion), channel_id=1, source_target_pairs={{0,1},{1,0},{2,3},{3,2},{4,5},{5,4},{6,7},{7,6},{8,9},{9,8},{10,11... | collective-permute-start | bytes 1769480 | tf_op jit(solution)/shard_map/ppermute | solution.py:27
  189.4 17.3 %collective-permute-start.18 = (bf16[2,384,384]{2,1,0:T(8,128)(2,1)}, bf16[2,384,384]{2,1,0:T(8,128)(2,1)}, u32[]{:S(2)}, u32[]{:S(2)}) collective-permute-start(bf16[2,384,384]{2,1,0:T(8,128)(2,1)} %fusion.2), channel_id=1, source_target_pairs={{0,4},{2,6},{4,0},{6,2},{8,12},{10,14},{12,8},{14,10},{16,20},{18,... | collective-permute-start | bytes 1769480 | tf_op jit(solution)/shard_map/ppermute | solution.py:23
  190.1 27.5 %collective-permute-start.17 = (bf16[2,192,768]{2,1,0:T(8,128)(2,1)}, bf16[2,192,768]{2,1,0:T(8,128)(2,1)}, u32[]{:S(2)}, u32[]{:S(2)}) collective-permute-start(bf16[2,192,768]{2,1,0:T(8,128)(2,1)} %fusion.3), channel_id=1, source_target_pairs={{0,4},{2,6},{4,0},{6,2},{8,12},{10,14},{12,8},{14,10},{16,20},{18,... | collective-permute-start | bytes 1769480 | tf_op jit(solution)/shard_map/ppermute | solution.py:23
  194.0 54.2 %collective-permute-start.16 = (bf16[2,2,4,96,384]{4,3,2,1,0:T(8,128)(2,1)S(1)}, bf16[2,2,4,96,384]{4,3,2,1,0:T(8,128)(2,1)}, u32[]{:S(2)}, u32[]{:S(2)}) collective-permute-start(bf16[2,2,4,96,384]{4,3,2,1,0:T(8,128)(2,1)S(1)} %add_convert_fusion), channel_id=1, source_target_pairs={{0,1},{1,0},{2,3},{3,2},{4,5},{5,4},{6,7},{7,6},{8,9},{9,8},{10,11... | collective-permute-start | bytes 3538952 | tf_op jit(solution)/shard_map/ppermute | solution.py:27
  227.3 21.0 %collective-permute-start.20 = (bf16[2,2,4,96,384]{4,3,2,1,0:T(8,128)(2,1)}, bf16[2,2,4,96,384]{4,3,2,1,0:T(8,128)(2,1)S(1)}, u32[]{:S(2)}, u32[]{:S(2)}) collective-permute-start(bf16[2,2,4,96,384]{4,3,2,1,0:T(8,128)(2,1)} %bitcast.93), channel_id=1, source_target_pairs={{0,2},{2,0},{4,6},{6,4},{8,10},{10,8},{12,14},{14,12},{16,18},{18,... | collective-permute-start | bytes 3538952 | tf_op jit(solution)/shard_map/ppermute | solution.py:23
  227.3 9.8 %collective-permute-start.22 = (bf16[384,384]{1,0:T(8,128)(2,1)S(1)}, bf16[384,384]{1,0:T(8,128)(2,1)S(1)}, u32[]{:S(2)}, u32[]{:S(2)}) collective-permute-start(bf16[384,384]{1,0:T(8,128)(2,1)S(1)} %fusion.13), channel_id=1, source_target_pairs={{0,8},{2,10},{4,12},{6,14},{8,0},{10,2},{12,4},{14,6},{16,24},{18,... | collective-permute-start | bytes 884744 | tf_op jit(solution)/shard_map/ppermute | solution.py:23
  228.9 17.9 %collective-permute-start.21 = (bf16[192,768]{1,0:T(8,128)(2,1)S(1)}, bf16[192,768]{1,0:T(8,128)(2,1)S(1)}, u32[]{:S(2)}, u32[]{:S(2)}) collective-permute-start(bf16[192,768]{1,0:T(8,128)(2,1)S(1)} %fusion.12), channel_id=1, source_target_pairs={{0,8},{2,10},{4,12},{6,14},{8,0},{10,2},{12,4},{14,6},{16,24},{18,... | collective-permute-start | bytes 884744 | tf_op jit(solution)/shard_map/ppermute | solution.py:23
  229.3 33.0 %collective-permute-start.24 = (f32[6912]{0:T(1024)}, f32[6912]{0:T(1024)}, u32[]{:S(2)}, u32[]{:S(2)}) collective-permute-start(f32[6912]{0:T(1024)} %pad_maximum_fusion.3), channel_id=1, source_target_pairs={{0,1},{1,0},{2,3},{3,2},{4,5},{5,4},{6,7},{7,6},{8,9},{9,8},{10,11... | collective-permute-start | bytes 82952 | tf_op jit(solution)/shard_map/ppermute | solution.py:27
  238.4 29.8 %collective-permute-start.26 = (bf16[384,384]{1,0:T(8,128)(2,1)S(1)}, bf16[384,384]{1,0:T(8,128)(2,1)S(1)}, u32[]{:S(2)}, u32[]{:S(2)}) collective-permute-start(bf16[384,384]{1,0:T(8,128)(2,1)S(1)} %fusion.11), channel_id=1, source_target_pairs={{0,16},{2,18},{4,20},{6,22},{8,24},{10,26},{12,28},{14,30},{16,0},... | collective-permute-start | bytes 884744 | tf_op jit(solution)/shard_map/ppermute | solution.py:23
  250.0 15.0 %collective-permute-start.23 = (bf16[2,4,96,384]{3,2,1,0:T(8,128)(2,1)S(1)}, bf16[2,4,96,384]{3,2,1,0:T(8,128)(2,1)S(1)}, u32[]{:S(2)}, u32[]{:S(2)}) collective-permute-start(bf16[2,4,96,384]{3,2,1,0:T(8,128)(2,1)S(1)} %fusion.4), channel_id=1, source_target_pairs={{0,4},{2,6},{4,0},{6,2},{8,12},{10,14},{12,8},{14,10},{16,20},{18,... | collective-permute-start | bytes 1769480 | tf_op jit(solution)/shard_map/ppermute | solution.py:23
  266.2 15.6 %collective-permute-start.25 = (bf16[4,96,384]{2,1,0:T(8,128)(2,1)S(1)}, bf16[4,96,384]{2,1,0:T(8,128)(2,1)S(1)}, u32[]{:S(2)}, u32[]{:S(2)}) collective-permute-start(bf16[4,96,384]{2,1,0:T(8,128)(2,1)S(1)} %fusion.7), channel_id=1, source_target_pairs={{0,8},{2,10},{4,12},{6,14},{8,0},{10,2},{12,4},{14,6},{16,24},{18,... | collective-permute-start | bytes 884744 | tf_op jit(solution)/shard_map/ppermute | solution.py:23
  266.3 16.8 %collective-permute-start.29 = (bf16[192,768]{1,0:T(8,128)(2,1)S(1)}, bf16[192,768]{1,0:T(8,128)(2,1)S(1)}, u32[]{:S(2)}, u32[]{:S(2)}) collective-permute-start(bf16[192,768]{1,0:T(8,128)(2,1)S(1)} %fusion.9), channel_id=1, source_target_pairs={{0,16},{2,18},{4,20},{6,22},{8,24},{10,26},{12,28},{14,30},{16,0},... | collective-permute-start | bytes 884744 | tf_op jit(solution)/shard_map/ppermute | solution.py:23
  268.3 20.3 %collective-permute-start.30 = (bf16[384,384]{1,0:T(8,128)(2,1)S(1)}, bf16[384,384]{1,0:T(8,128)(2,1)S(1)}, u32[]{:S(2)}, u32[]{:S(2)}) collective-permute-start(bf16[384,384]{1,0:T(8,128)(2,1)S(1)} %add_convert_fusion.8), channel_id=1, source_target_pairs={{0,4},{2,6},{4,0},{6,2},{8,12},{10,14},{12,8},{14,10},{16,20},{18,... | collective-permute-start | bytes 884744 | tf_op jit(solution)/shard_map/ppermute | solution.py:23
  269.6 17.4 %collective-permute-start.28 = (bf16[384,384]{1,0:T(8,128)(2,1)S(1)}, bf16[384,384]{1,0:T(8,128)(2,1)S(1)}, u32[]{:S(2)}, u32[]{:S(2)}) collective-permute-start(bf16[384,384]{1,0:T(8,128)(2,1)S(1)} %add_convert_fusion.8), channel_id=1, source_target_pairs={{0,8},{2,10},{4,12},{6,14},{8,0},{10,2},{12,4},{14,6},{16,24},{18,... | collective-permute-start | bytes 884744 | tf_op jit(solution)/shard_map/ppermute | solution.py:23
  287.0 7.9 %collective-permute-start.31 = (bf16[384,384]{1,0:T(8,128)(2,1)S(1)}, bf16[384,384]{1,0:T(8,128)(2,1)S(1)}, u32[]{:S(2)}, u32[]{:S(2)}) collective-permute-start(bf16[384,384]{1,0:T(8,128)(2,1)S(1)} %collective-permute-done.28), channel_id=1, source_target_pairs={{0,4},{2,6},{4,0},{6,2},{8,12},{10,14},{12,8},{14,10},{16,20},{18,... | collective-permute-start | bytes 884744 | tf_op jit(solution)/shard_map/ppermute | solution.py:23
  295.1 12.1 %collective-permute-start.32 = (bf16[4,384,384]{2,1,0:T(8,128)(2,1)S(1)}, bf16[4,384,384]{2,1,0:T(8,128)(2,1)}, u32[]{:S(2)}, u32[]{:S(2)}) collective-permute-start(bf16[4,384,384]{2,1,0:T(8,128)(2,1)S(1)} %pad_maximum_fusion.refs_0_), channel_id=1, source_target_pairs={{0,2},{2,0},{4,6},{6,4},{8,10},{10,8},{12,14},{14,12},{16,18},{18,... | collective-permute-start | bytes 3538952 | tf_op jit(solution)/shard_map/ppermute | solution.py:23
  295.2 10.6 %collective-permute-start.37 = (bf16[192,768]{1,0:T(8,128)(2,1)S(1)}, bf16[192,768]{1,0:T(8,128)(2,1)S(1)}, u32[]{:S(2)}, u32[]{:S(2)}) collective-permute-start(bf16[192,768]{1,0:T(8,128)(2,1)S(1)} %add_convert_fusion.7), channel_id=1, source_target_pairs={{0,8},{2,10},{4,12},{6,14},{8,0},{10,2},{12,4},{14,6},{16,24},{18,... | collective-permute-start | bytes 884744 | tf_op jit(solution)/shard_map/ppermute | solution.py:23
  295.3 2.7 collective-permute-start.34
  298.0 17.8 %collective-permute-start.35 = (f32[6912]{0:T(1024)S(1)}, f32[6912]{0:T(1024)S(1)}, u32[]{:S(2)}, u32[]{:S(2)}) collective-permute-start(f32[6912]{0:T(1024)S(1)} %add.190), channel_id=1, source_target_pairs={{0,4},{2,6},{4,0},{6,2},{8,12},{10,14},{12,8},{14,10},{16,20},{18,... | collective-permute-start | bytes 82952 | tf_op jit(solution)/shard_map/ppermute | solution.py:23
  299.6 16.3 %collective-permute-start.38 = (bf16[192,768]{1,0:T(8,128)(2,1)S(1)}, bf16[192,768]{1,0:T(8,128)(2,1)S(1)}, u32[]{:S(2)}, u32[]{:S(2)}) collective-permute-start(bf16[192,768]{1,0:T(8,128)(2,1)S(1)} %add_convert_fusion.7), channel_id=1, source_target_pairs={{0,4},{2,6},{4,0},{6,2},{8,12},{10,14},{12,8},{14,10},{16,20},{18,... | collective-permute-start | bytes 884744 | tf_op jit(solution)/shard_map/ppermute | solution.py:23
  300.1 15.7 %collective-permute-start.27 = (bf16[4,96,384]{2,1,0:T(8,128)(2,1)S(1)}, bf16[4,96,384]{2,1,0:T(8,128)(2,1)S(1)}, u32[]{:S(2)}, u32[]{:S(2)}) collective-permute-start(bf16[4,96,384]{2,1,0:T(8,128)(2,1)S(1)} %fusion.6), channel_id=1, source_target_pairs={{0,16},{2,18},{4,20},{6,22},{8,24},{10,26},{12,28},{14,30},{16,0},... | collective-permute-start | bytes 884744 | tf_op jit(solution)/shard_map/ppermute | solution.py:23
  305.8 10.1 %collective-permute-start.39 = (bf16[192,768]{1,0:T(8,128)(2,1)S(1)}, bf16[192,768]{1,0:T(8,128)(2,1)S(1)}, u32[]{:S(2)}, u32[]{:S(2)}) collective-permute-start(bf16[192,768]{1,0:T(8,128)(2,1)S(1)} %collective-permute-done.37), channel_id=1, source_target_pairs={{0,4},{2,6},{4,0},{6,2},{8,12},{10,14},{12,8},{14,10},{16,20},{18,... | collective-permute-start | bytes 884744 | tf_op jit(solution)/shard_map/ppermute | solution.py:23
  316.1 3.7 %collective-permute-start.40 = (bf16[4,192,768]{2,1,0:T(8,128)(2,1)S(1)}, bf16[4,192,768]{2,1,0:T(8,128)(2,1)}, u32[]{:S(2)}, u32[]{:S(2)}) collective-permute-start(bf16[4,192,768]{2,1,0:T(8,128)(2,1)S(1)} %pad_maximum_fusion.1.refs_0_), channel_id=1, source_target_pairs={{0,2},{2,0},{4,6},{6,4},{8,10},{10,8},{12,14},{14,12},{16,18},{18,... | collective-permute-start | bytes 3538952 | tf_op jit(solution)/shard_map/ppermute | solution.py:23
  316.1 7.6 %collective-permute-start.36 = (f32[6912]{0:T(1024)S(1)}, f32[6912]{0:T(1024)S(1)}, u32[]{:S(2)}, u32[]{:S(2)}) collective-permute-start(f32[6912]{0:T(1024)S(1)} %add.191), channel_id=1, source_target_pairs={{0,8},{2,10},{4,12},{6,14},{8,0},{10,2},{12,4},{14,6},{16,24},{18,... | collective-permute-start | bytes 82952 | tf_op jit(solution)/shard_map/ppermute | solution.py:23
  316.2 16.3 %collective-permute-start.41 = (bf16[4,96,384]{2,1,0:T(8,128)(2,1)S(1)}, bf16[4,96,384]{2,1,0:T(8,128)(2,1)S(1)}, u32[]{:S(2)}, u32[]{:S(2)}) collective-permute-start(bf16[4,96,384]{2,1,0:T(8,128)(2,1)S(1)} %add_convert_fusion.6), channel_id=1, source_target_pairs={{0,4},{2,6},{4,0},{6,2},{8,12},{10,14},{12,8},{14,10},{16,20},{18,... | collective-permute-start | bytes 884744 | tf_op jit(solution)/shard_map/ppermute | solution.py:23
  317.8 9.0 %collective-permute-start.33 = (bf16[4,96,384]{2,1,0:T(8,128)(2,1)S(1)}, bf16[4,96,384]{2,1,0:T(8,128)(2,1)S(1)}, u32[]{:S(2)}, u32[]{:S(2)}) collective-permute-start(bf16[4,96,384]{2,1,0:T(8,128)(2,1)S(1)} %add_convert_fusion.6), channel_id=1, source_target_pairs={{0,8},{2,10},{4,12},{6,14},{8,0},{10,2},{12,4},{14,6},{16,24},{18,... | collective-permute-start | bytes 884744 | tf_op jit(solution)/shard_map/ppermute | solution.py:23
  326.8 8.2 %collective-permute-start.42 = (bf16[4,96,384]{2,1,0:T(8,128)(2,1)S(1)}, bf16[4,96,384]{2,1,0:T(8,128)(2,1)S(1)}, u32[]{:S(2)}, u32[]{:S(2)}) collective-permute-start(bf16[4,96,384]{2,1,0:T(8,128)(2,1)S(1)} %collective-permute-done.33), channel_id=1, source_target_pairs={{0,4},{2,6},{4,0},{6,2},{8,12},{10,14},{12,8},{14,10},{16,20},{18,... | collective-permute-start | bytes 884744 | tf_op jit(solution)/shard_map/ppermute | solution.py:23
  327.7 4.8 %collective-permute-start.43 = (f32[6912]{0:T(1024)S(1)}, f32[6912]{0:T(1024)S(1)}, u32[]{:S(2)}, u32[]{:S(2)}) collective-permute-start(f32[6912]{0:T(1024)S(1)} %add.192), channel_id=1, source_target_pairs={{0,16},{2,18},{4,20},{6,22},{8,24},{10,26},{12,28},{14,30},{16,0},... | collective-permute-start | bytes 82952 | tf_op jit(solution)/shard_map/ppermute | solution.py:23
  335.2 2.9 collective-permute-start.44
  (32 other events, 216.5 us)
